TPU v7x, 32 devices: a whole 2x2x4 slice. The times are simulated.
32 devices in a mesh: wave: 4 (over z), tile: 8 (over y, x, core).
Axes of the slice: x: 2, y: 2, z: 4, core: 2. Of those that a mesh axis runs over, the one named last changes fastest.
Arguments:
- spectral: bfloat16 [640, 2, 64, 1281], P('wave', None, 'tile'), may hold values from -0.083496094 to 0.083496094
- legendre: bfloat16 [640, 8, 1281], P('wave'), may hold values from -0.25 to 0.25
- pair_ids: int32 [640], replicated, may hold values from 0 to 639, each once
Outputs:
- spectral_out: bfloat16 [640, 2, 64, 1281], P('wave', None, 'tile')
Inputs may be any that keep to these rules, and one draw needn't show every extreme that they name: A permutation: each pair 0 to 639 appears once; slot s of spectral, legendre and spectral_out holds wavenumbers pair_ids[s] and 1279 - pair_ids[s].
All inputs are finite; a program needn't handle non-finite values.
Results may differ from a plain program's by a relative error of at most 0.0072.
Values may be sent and summed in bfloat16 or wider, within the bound.
A program may use at most 64 MiB of HBM per device.

v0:
```python
import math

import jax
import jax.numpy as jnp
from jax import lax
from jax.sharding import PartitionSpec as P

MW = 1280
HALF_LATS = 1280
PAIRS = 640
NPTS = 5156


def build_table(wavenumbers, local_index, length, inside, synthesis):
    phase_step = wavenumbers[:, None] * local_index[None, :] % length[None, :]
    angles = 2.0 * math.pi * phase_step.astype(jnp.float32) / length[None, :].astype(jnp.float32)
    keep_mask = (2 * wavenumbers[:, None] < length[None, :]) & inside[None, :]
    if synthesis:
        factor = jnp.where(wavenumbers == 0, 1.0, 2.0).astype(jnp.float32)[:, None]
    else:
        factor = jnp.ones((wavenumbers.shape[0], 1), jnp.float32)
    cosine = jnp.where(keep_mask, factor * jnp.cos(angles), 0.0)
    sine_part = jnp.where(keep_mask, -factor * jnp.sin(angles), 0.0)
    return jnp.concatenate([cosine, sine_part], axis=0).astype(jnp.bfloat16)


def cycle_lengths(pair_number, pair_total):
    polar_cycle = pair_number * (HALF_LATS // 2) // pair_total
    cycle_index = jnp.stack([polar_cycle, HALF_LATS - 1 - polar_cycle])
    return (cycle_index, 20 + 4 * cycle_index)


def point_layout(points, cycle_len):
    second = points >= cycle_len[0]
    local_index = points - jnp.where(second, cycle_len[0], 0)
    length = jnp.where(second, cycle_len[1], cycle_len[0])
    inside = points < cycle_len[0] + cycle_len[1]
    return (second, local_index, length, inside)


def cycle_scale(cycle_index, cycle_len, lat_count):
    angles = math.pi * (cycle_index.astype(jnp.float32) + 0.5) / (2.0 * HALF_LATS)
    return 40.0 * jnp.sin(angles) / jnp.sqrt(lat_count * cycle_len.astype(jnp.float32))


def grid_products(grid_values):
    layer_count = grid_values.shape[0] // 4
    nodal_samples = grid_values.astype(jnp.float32).reshape(4, layer_count, grid_values.shape[1])
    zonal_velocity = nodal_samples[0]
    meridional_velocity = nodal_samples[1]
    thermal_state = nodal_samples[2]
    moisture_ratio = nodal_samples[3]
    gravity_surface_altitude = lax.cumsum(thermal_state, axis=0, reverse=True) / math.sqrt(
        layer_count
    )
    motion_squared_half = (
        0.5 * (zonal_velocity * zonal_velocity + meridional_velocity * meridional_velocity)
        + gravity_surface_altitude
    )
    joined_variables = jnp.stack(
        [
            motion_squared_half,
            zonal_velocity * thermal_state,
            meridional_velocity * thermal_state,
            zonal_velocity * moisture_ratio,
        ]
    )
    return joined_variables.reshape(grid_values.shape).astype(jnp.bfloat16)


def local(spectral, legendre, pair_ids):
    slot_count = spectral.shape[0]
    col_here = spectral.shape[2]
    row_total = spectral.shape[3]
    lat_count = legendre.shape[1]
    tile_total = lax.axis_size("tile")
    tile_points = (NPTS + tile_total - 1) // tile_total
    block_tiles = tile_total
    while block_tiles * tile_points > 1536 and block_tiles % 2 == 0:
        block_tiles = block_tiles // 2
    zero_value = jnp.zeros((), jnp.bfloat16)
    wave_here = lax.axis_index("wave")
    slot_ids = lax.dynamic_slice_in_dim(pair_ids, wave_here * slot_count, slot_count)
    row_index = lax.broadcasted_iota(jnp.int32, (slot_count, row_total), 1)
    upper_rows = (row_index >= (MW - slot_ids)[:, None])[:, None, None, :]
    halves = jnp.stack(
        [jnp.where(upper_rows, zero_value, spectral), jnp.where(upper_rows, spectral, zero_value)],
        axis=1,
    )
    coefficients = lax.dot_general(
        legendre,
        halves.reshape(slot_count, 4 * col_here, row_total),
        (((2,), (2,)), ((0,), (0,))),
        preferred_element_type=jnp.float32,
    )
    coefficients = coefficients.reshape(slot_count, lat_count, 2, 2, col_here).astype(jnp.bfloat16)
    fourier = lax.all_to_all(coefficients, "wave", split_axis=1, concat_axis=0, tiled=True)
    cycle_index, cycle_len = cycle_lengths(wave_here, lat_count // 2)
    scales = cycle_scale(cycle_index, cycle_len, lat_count)
    wavenumbers = jnp.concatenate([pair_ids, MW - 1 - pair_ids])
    tile_start = lax.axis_index("tile") * tile_points
    own_points = tile_start + lax.iota(jnp.int32, tile_points)
    second, local_index, length, inside = point_layout(own_points, cycle_len)
    synth_table = build_table(wavenumbers, local_index, length, inside, True)
    shard_piece = lax.all_gather(fourier, "tile", axis=4, tiled=True)
    col_count = shard_piece.shape[4]
    matrix = jnp.transpose(shard_piece, (1, 4, 3, 2, 0)).reshape(2 * col_count, 4 * PAIRS)
    result = jnp.dot(matrix, synth_table, preferred_element_type=jnp.float32).reshape(
        2, col_count, tile_points
    )
    grid_values = jnp.where(second[None, :], result[1], result[0]).astype(jnp.bfloat16)
    product = grid_products(grid_values)
    second, local_index, length, inside = point_layout(own_points, cycle_len)
    anal_table = build_table(wavenumbers, local_index, length, inside, False)
    split_rows = jnp.concatenate(
        [
            jnp.where(second[None, :], zero_value, product),
            jnp.where(second[None, :], product, zero_value),
        ],
        axis=0,
    )
    result = lax.dot_general(
        split_rows, anal_table, (((1,), (1,)), ((), ())), preferred_element_type=jnp.float32
    )
    result = result.reshape(2, col_here * lax.axis_size("tile"), 4 * PAIRS) * scales[:, None, None]
    spectra_sum = lax.psum_scatter(
        jnp.transpose(result, (1, 0, 2)), "tile", scatter_dimension=0, tiled=True
    )
    spectra_here = spectra_sum.astype(jnp.bfloat16)
    outgoing = jnp.transpose(spectra_here.reshape(col_here, 2, 2, 2, PAIRS), (4, 1, 3, 2, 0))
    returned = lax.all_to_all(outgoing, "wave", split_axis=0, concat_axis=1, tiled=True)
    result = lax.dot_general(
        returned.reshape(slot_count, lat_count, 4 * col_here),
        legendre,
        (((1,), (1,)), ((0,), (0,))),
        preferred_element_type=jnp.float32,
    )
    result = result.reshape(slot_count, 2, 2, col_here, row_total)
    return jnp.where(upper_rows, result[:, 1], result[:, 0]).astype(jnp.bfloat16)


def solution(mesh):
    placed = (P("wave", None, "tile", None), P("wave", None, None), P())
    return jax.shard_map(
        local, mesh=mesh, in_specs=placed, out_specs=P("wave", None, "tile", None), check_vma=False
    )
```

profile of v0, /device:TPU:0, one launch (start us, length us, event | category | flops | bytes accessed | tf_op | source)
XLA Modules:
  0.0 187.6 jit_solution(1341078424027038657)
XLA Ops:
  6.5 0.8 dynamic-slice_subtract_fusion
  7.3 0.2 iota_compare_fusion
  7.5 4.8 %select_bitcast_fusion.1 = (bf16[160,1,2,8,1281]{4,3,2,0,1:T(8,128)(2,1)S(1)}, bf16[160,1,2,8,1281]{4,3,2,0,1:T(8,128)(2,1)S(1)}) fusion(bf16[160,2,8,1281]{3,2,1,0:T(8,128)(2,1)} %param.5, pred[160,1281]{1,0:T(8,128)(4,1)S(1)} %iota_compare_fusion), kind=kLoop, calls=%fused_computation.6 | loop fusion | flops 6558720 | bytes 19881120 | tf_op jit(solution)/shard_map/stack | solution.py:86
  12.4 1.9 pad_maximum_fusion
  14.2 3.5 %copy.77 = bf16[160,2,2,8,1281]{4,3,2,1,0:T(8,128)(2,1)S(1)} copy(bf16[160,2,2,8,1281]{4,3,2,0,1:T(8,128)(2,1)S(1)} %pad_maximum_fusion) | data formatting | bytes 26234880 | tf_op jit(solution)/shard_map/stack | solution.py:86
  17.8 0.0 copy-start
  17.8 6.2 %fusion.19 = bf16[160,8,32]{2,1,0:T(8,128)(2,1)S(1)} fusion(bf16[160,32,1281]{2,1,0:T(8,128)(2,1)S(1)} %bitcast.60, bf16[160,8,1281]{2,1,0:T(8,128)(2,1)} %param.6), kind=kOutput, calls=%fused_computation.33 | convolution fusion | flops 104980480 | bytes 16478720 | tf_op jit(solution)/shard_map/dot_general | solution.py:90
  24.0 0.9 copy.78
  24.9 6.3 %all-to-all-start = ((bf16[160,8,2,2,8]{0,4,3,2,1:T(8,128)(2,1)}), bf16[160,8,2,2,8]{0,4,3,2,1:T(8,128)(2,1)S(1)}, u32[]{:S(2)}, u32[]{:S(2)}) async-start(bf16[160,8,2,2,8]{0,4,3,2,1:T(8,128)(2,1)} %bitcast.7), calls=%async_computation | async-start | bytes 262144 | tf_op jit(solution)/shard_map/all_to_all | solution.py:97
  31.2 0.0 reduce-scatter.2.cloned.1.call-start
  31.3 0.0 copy-done
  31.3 0.1 multiply_add_fusion
  31.4 0.6 fusion.37
  33.2 1.3 compare_reduce_fusion
  34.5 0.7 select_subtract_fusion
  35.2 1.3 fusion.32
  36.4 1.3 broadcast_select_fusion
  37.7 0.7 fusion.30
  38.4 57.9 %select_convert_fusion.3 = (bf16[1280,645]{1,0:T(8,128)(2,1)}, bf16[1280,645]{1,0:T(8,128)(2,1)}, bf16[1280,645]{1,0:T(8,128)(2,1)}, bf16[1280,645]{1,0:T(8,128)(2,1)}) fusion(f32[1280]{0:T(1024)S(1)} %get-tuple-element.18, s32[645]{0:T(1024)S(1)} %get-tuple-element.24, s32[1280]{0:T(1024)S(1)} %get-tuple-element.21, f32[645]{0:T(1024)S(1)} %get-tuple-element.25, ...), kind=kLoop, calls=%fused_computation.22 | loop fusion | flops 19814400 | bytes 6636890 | tf_op jit(solution)/shard_map/convert.10
  96.3 0.1 rsqrt_multiply_fusion
  96.4 0.0 all-to-all-done
  96.4 0.1 copy.94
  96.5 0.1 all_to_all.27
  96.7 10.6 %all_gather.3 = bf16[640,2,2,2,64]{0,4,3,2,1:T(8,128)(2,1)S(1)} all-gather(bf16[640,2,2,2,8]{0,4,3,2,1:T(8,128)(2,1)S(1)} %all_to_all.27), channel_id=1, replica_groups=mesh['wave'=4,'tile'=8] {'tile'}, dimensions={4}, use_global_device_ids=true | all-gather | bytes 737280 | tf_op jit(solution)/shard_map/all_gather | solution.py:105
  107.2 0.7 copy.80
  107.9 0.4 reshape.162
  108.3 2.8 %fusion.5 = bf16[128,645]{1,0:T(8,128)(2,1)S(1)} fusion(bf16[128,2560]{1,0:T(8,128)(2,1)S(1)} %reshape.162, bf16[1280,645]{1,0:T(8,128)(2,1)} %get-tuple-element.16, bf16[1280,645]{1,0:T(8,128)(2,1)} %get-tuple-element.14), kind=kOutput, calls=%fused_computation.11 | convolution fusion | flops 429312000 | bytes 4122880 | tf_op jit(solution)/shard_map/dot_general | solution.py:108
  111.2 0.1 reduce_window_sum.10
  111.4 3.5 %fusion.9 = f32[128,2560]{1,0:T(8,128)S(1)} fusion(bf16[1280,645]{1,0:T(8,128)(2,1)} %get-tuple-element.17, bf16[1280,645]{1,0:T(8,128)(2,1)} %get-tuple-element.15, bf16[64,645]{1,0:T(8,128)(2,1)S(1)} %get-tuple-element.13, bf16[64,645]{1,0:T(8,128)(2,1)S(1)} %get-tuple-element.12), kind=kOutput, calls=%fused_computation.15 | convolution fusion | flops 429642240 | bytes 4778240 | tf_op jit(solution)/shard_map/dot_general | solution.py:122
  115.0 1.3 multiply_bitcast_fusion
  116.2 0.0 reduce-scatter.2.cloned.1.call-update
  116.3 37.9 %reduce-scatter.2.cloned.1.call-done = f32[8,2,2560]{2,0,1:T(8,128)} async-done(((f32[64,2,2560]{2,0,1:T(8,128)}), f32[8,2,2560]{2,0,1:T(8,128)}) %reduce-scatter.2.cloned.1.call-update) | async-done | bytes 163856 | tf_op jit(solution)/shard_map/reduce_scatter | solution.py:126
  154.1 0.9 convert_element_type.64
  155.1 1.0 copy.83
  156.1 1.4 reshape.169
  157.5 10.2 %all_to_all.33 = bf16[4,2,5120]{2,1,0:T(2,128)(2,1)S(1)} all-to-all(bf16[4,2,5120]{2,1,0:T(2,128)(2,1)S(1)} %reshape.169), channel_id=1, replica_groups=mesh['wave'=4,'tile'=8] {'wave'}, dimensions={0} | all-to-all | bytes 163840 | tf_op jit(solution)/shard_map/all_to_all | solution.py:131
  167.6 1.5 reshape.170
  169.2 1.8 copy.90
  171.0 0.2 copy.86
  171.2 5.7 %fusion.38 = bf16[160,32,1281]{2,1,0:T(8,128)(2,1)S(1)} fusion(bf16[160,8,32]{2,1,0:T(8,128)(2,1)S(1)} %copy.86, bf16[160,8,1281]{2,1,0:T(8,128)(2,1)} %param.6), kind=kOutput, calls=%fused_computation.76 | convolution fusion | flops 104939520 | bytes 16478720 | tf_op jit(solution)/shard_map/dot_general | solution.py:132
  176.9 3.9 %fusion.1 = bf16[160,2,8,1281]{3,2,1,0:T(8,128)(2,1)} fusion(bf16[160,2,2,8,1281]{4,3,2,1,0:T(8,128)(2,1)S(1)} %bitcast.59, pred[160,1281]{1,0:T(8,128)(4,1)S(1)} %iota_compare_fusion), kind=kLoop, calls=%fused_computation.2 | loop fusion | flops 3279360 | bytes 19881120 | tf_op jit(solution)/shard_map/convert_element_type | solution.py:139
  (10 shorter events, 0.2 us)
Async XLA Ops:
  17.8 13.5 %copy-start = (s32[640]{0:T(1024)S(1)}, s32[640]{0:T(1024)}, u32[]{:S(2)}) copy-start(s32[640]{0:T(1024)} %param.7) | copy-start | bytes 7684
  24.9 71.5 %all-to-all-start = ((bf16[160,8,2,2,8]{0,4,3,2,1:T(8,128)(2,1)}), bf16[160,8,2,2,8]{0,4,3,2,1:T(8,128)(2,1)S(1)}, u32[]{:S(2)}, u32[]{:S(2)}) async-start(bf16[160,8,2,2,8]{0,4,3,2,1:T(8,128)(2,1)} %bitcast.7), calls=%async_computation | async-start | bytes 262144 | tf_op jit(solution)/shard_map/all_to_all | solution.py:97
  31.2 122.9 %reduce-scatter.2.cloned.1.call-start = ((), (), s32[]{:S(2)}) async-start(), calls=%async_computation.3 | async-start | bytes 1474560 | tf_op jit(solution)/shard_map/reduce_scatter | solution.py:126
Sparse Core Ops, SparseCore 0:
  116.4 37.6 reduce-scatter.1
where the time goes:
time: 188 us
  other arithmetic  77.2 us (41%)
  waiting for transfers between devices  37.9 us (20%)
  blocking collectives  20.8 us (11%)
  matrix products  18.2 us (10%)
  between operations  14.9 us (8%)
  local copies, waits for them, and re-layouts  12.4 us (7%)
  starting transfers between devices  6.35 us (3%)
    another operation x1, other arithmetic  57.9 us
    reduce_scatter x1, waiting for transfers between devices, local(): lax.psum_scatter(jnp.transpose(result, (1, 0, 2)), 'tile', scatter_dimens...  37.9 us
    all_gather x1, blocking collectives, local(): shard_piece = lax.all_gather(fourier, 'tile', axis=4, tiled=True)  10.6 us
    all_to_all x1, blocking collectives, local(): lax.all_to_all(outgoing, 'wave', split_axis=0, concat_axis=1, tiled=True)  10.2 us
    another operation x2, other arithmetic, local(): jnp.stack([jnp.where(upper_rows, zero_value, spectral), jnp.where(upper_r...  6.71 us
    all_to_all x1, starting transfers between devices, local(): lax.all_to_all(coefficients, 'wave', split_axis=1, concat_axis=0, tiled=T...  6.35 us
    dot_general x1, matrix products, local(): lax.dot_general(legendre, halves.reshape(slot_count, 4 * col_here, row_to...  6.19 us
    dot_general x1, matrix products, local(): lax.dot_general(returned.reshape(slot_count, lat_count, 4 * col_here), le...  5.68 us
  transfers between devices with their start and end apart: 2, of which 1 were waited for; matrix products, arithmetic and copies ran while one was open for 34% of the time, Pallas kernels for 0%

commit v1 on v0

v1 whole, which is shorter than its diff:
```python
import functools
import math

import jax
import jax.numpy as jnp
from jax import lax
from jax.sharding import PartitionSpec as P

MW = 1280
HALF_LATS = 1280
PAIRS = 640
NPTS = 5156
LANES = 128
RADIX = 32

F32 = jnp.float32
BF16 = jnp.bfloat16


def cycle_lengths(pair_number, pair_total):
    polar_cycle = pair_number * (HALF_LATS // 2) // pair_total
    cycle_index = jnp.stack([polar_cycle, HALF_LATS - 1 - polar_cycle])
    return (cycle_index, 20 + 4 * cycle_index)


def cycle_scale(cycle_index, cycle_len, lat_count):
    angles = math.pi * (cycle_index.astype(F32) + 0.5) / (2.0 * HALF_LATS)
    return 40.0 * jnp.sin(angles) / jnp.sqrt(lat_count * cycle_len.astype(F32))


def trig(wavenumbers, local_index, length):
    phase = (wavenumbers[:, None] * local_index[None, :]) % length[None, :]
    angles = 2.0 * math.pi * phase.astype(F32) / length[None, :].astype(F32)
    return jnp.cos(angles), jnp.sin(angles)


def tables(local_index, length):
    outer = MW // 2 // RADIX
    a_cos, a_sin = trig(2 * RADIX * lax.iota(jnp.int32, outer), local_index, length)
    b_cos, b_sin = trig(lax.iota(jnp.int32, 2 * RADIX), local_index, length)
    pts = local_index.shape[0]
    b_cos = b_cos.reshape(RADIX, 2, pts).transpose(1, 0, 2)[:, None]
    b_sin = b_sin.reshape(RADIX, 2, pts).transpose(1, 0, 2)[:, None]
    a_cos, a_sin = a_cos[None, :, None], a_sin[None, :, None]
    cos = (a_cos * b_cos - a_sin * b_sin).astype(BF16).reshape(2, MW // 2, pts)
    sin = (a_sin * b_cos + a_cos * b_sin).astype(BF16).reshape(2, MW // 2, pts)
    return cos, sin


def grid_products(grid_values):
    layer_count = grid_values.shape[0] // 4
    u, w, t, q = grid_values.astype(F32).reshape(4, layer_count, grid_values.shape[1])
    level = lax.iota(jnp.int32, layer_count)
    acc, rows = t[layer_count - 1], []
    rows.append(acc)
    for v in range(layer_count - 2, -1, -1):
        acc = acc + t[v]
        rows.append(acc)
    geo = jnp.stack(rows[::-1]) / math.sqrt(layer_count)
    energy = 0.5 * (u * u + w * w) + geo
    return jnp.stack([energy, u * t, w * t, u * q]).reshape(grid_values.shape).astype(BF16)


def local(spectral, legendre, pair_ids):
    slots, _, cols, row_total = spectral.shape
    lat_count = legendre.shape[1]
    tiles = lax.axis_size("tile")
    zero = jnp.zeros((), BF16)
    wave_here = lax.axis_index("wave")
    slot_ids = lax.dynamic_slice_in_dim(pair_ids, wave_here * slots, slots)
    row_index = lax.broadcasted_iota(jnp.int32, (slots, row_total), 1)
    upper = (row_index >= (MW - slot_ids)[:, None])[:, None, :]
    masked = jnp.concatenate(
        [jnp.where(upper, zero, legendre), jnp.where(upper, legendre, zero)], axis=1
    )
    spec = spectral.reshape(slots, 2 * cols, row_total)

    cycle_index, cycle_len = cycle_lengths(wave_here, lat_count // 2)
    scales = cycle_scale(cycle_index, cycle_len, lat_count)
    quarter = NPTS // 4
    step = tiles * LANES // math.gcd(4, tiles) if tiles * LANES // math.gcd(4, tiles) <= 512 else 512
    kpad = -(-quarter // step) * step
    k = lax.iota(jnp.int32, kpad)
    q0 = cycle_len[0] // 4
    second = k >= q0
    inside = k < quarter
    local_index = jnp.where(inside, k - jnp.where(second, q0, 0), 0)
    length = jnp.where(second, cycle_len[1], cycle_len[0])
    cos, sin = tables(local_index, length)

    half = MW // 2
    m_order = jnp.arange(MW, dtype=jnp.int32).reshape(half, 2).T
    quarter_m = half // 2
    m0, m1 = m_order[:, :quarter_m], m_order[:, quarter_m:]
    q_of = jnp.stack([m0, MW - 1 - m1]).reshape(2, half)
    hot = (pair_ids[None, :, None] == q_of[:, None, :]).astype(BF16)

    coefficients = lax.dot_general(
        masked, spec, (((2,), (2,)), ((0,), (0,))), preferred_element_type=F32
    ).astype(BF16).reshape(slots, 2, lat_count, 2 * cols)
    coefficients = coefficients.transpose(2, 1, 3, 0)
    fourier = lax.all_to_all(coefficients, "wave", split_axis=0, concat_axis=3, tiled=True)
    ordered = lax.dot_general(
        fourier, hot, (((3,), (1,)), ((1,), (0,))), preferred_element_type=F32
    )
    ordered = ordered.reshape(2, 2, 2, cols, 2, quarter_m).transpose(4, 2, 1, 3, 0, 5)
    ordered = ordered.reshape(2, 2, 2, cols, half)
    factor = jnp.where(m_order == 0, 1.0, 2.0).astype(F32)
    keep = 2 * m_order[:, None, :] < cycle_len[None, :, None]
    ordered = ordered * jnp.where(keep, factor[:, None, :], 0.0)[:, None, :, None, :]
    sign = jnp.where(m_order // 2 % 2 == 0, 1.0, -1.0).astype(F32)
    re, im = ordered[:, 0].reshape(2, 2 * cols, half), ordered[:, 1].reshape(2, 2 * cols, half)
    even_c = jnp.concatenate([re[0], re[0] * sign[0]]).astype(BF16)
    even_s = jnp.concatenate([-im[0], -im[0] * sign[0]]).astype(BF16)
    odd_c = jnp.concatenate([re[1], im[1] * sign[1]]).astype(BF16)
    odd_s = jnp.concatenate([-im[1], re[1] * sign[1]]).astype(BF16)
    dot = functools.partial(jnp.dot, preferred_element_type=F32)
    even = (dot(even_c, cos[0]) + dot(even_s, sin[0])).reshape(2, 2, cols, kpad)
    odd = (dot(odd_c, cos[1]) + dot(odd_s, sin[1])).reshape(2, 2, cols, kpad)
    even = jnp.where(second, even[:, 1], even[:, 0])
    odd = jnp.where(second, odd[:, 1], odd[:, 0])
    grid_values = jnp.stack(
        [even[0] + odd[0], even[1] - odd[1], even[0] - odd[0], even[1] + odd[1]], axis=1
    ).astype(BF16)
    grid_values = grid_values.reshape(cols, 4 * kpad)
    grid_values = lax.all_to_all(grid_values, "tile", split_axis=1, concat_axis=0, tiled=True)
    product = grid_products(grid_values)
    product = lax.all_to_all(product, "tile", split_axis=0, concat_axis=1, tiled=True)
    x = product.astype(F32).reshape(cols, 4, kpad)
    x = jnp.where(inside, x, 0.0)
    x0, x1, x2, x3 = x[:, 0], x[:, 1], x[:, 2], x[:, 3]
    def by_lat(a, b):
        both = jnp.stack([a, b])[:, None]
        return jnp.where(
            second == (lax.iota(jnp.int32, 2) == 1)[None, :, None, None], both, 0.0
        ).astype(BF16).reshape(4 * cols, kpad)
    even_in = by_lat((x0 + x2) + (x1 + x3), (x0 + x2) - (x1 + x3))
    odd_in = by_lat(x0 - x2, x1 - x3)
    nt = lambda a, b: lax.dot_general(
        a, b, (((1,), (1,)), ((), ())), preferred_element_type=F32
    ).reshape(2, 2, cols, half)
    ec, es = nt(even_in, cos[0]), nt(even_in, sin[0])
    oc, os_ = nt(odd_in, cos[1]), nt(odd_in, sin[1])
    pick = sign[0] > 0
    even_re = jnp.where(pick, ec[0], ec[1])
    even_im = -jnp.where(pick, es[0], es[1])
    odd_re = oc[0] - sign[1] * os_[1]
    odd_im = -os_[0] - sign[1] * oc[1]
    back = jnp.stack([jnp.stack([even_re, even_im]), jnp.stack([odd_re, odd_im])])
    back = back * jnp.where(keep, scales[None, :, None], 0.0)[:, None, :, None, :]
    back = back.astype(BF16).reshape(2, 2, 2, cols, 2, quarter_m).transpose(4, 2, 1, 3, 0, 5)
    back = back.reshape(2, 4 * cols, half)
    back = lax.dot_general(
        back, hot, (((2,), (2,)), ((0,), (0,))), preferred_element_type=F32
    ).astype(BF16)
    back = back.reshape(2, 2, 2 * cols, PAIRS).transpose(1, 0, 2, 3)
    returned = lax.all_to_all(back, "wave", split_axis=3, concat_axis=0, tiled=True)
    returned = returned.transpose(3, 2, 1, 0).reshape(slots, 2 * cols, 2 * lat_count)
    result = lax.dot_general(
        returned, masked, (((2,), (1,)), ((0,), (0,))), preferred_element_type=F32
    )
    return result.reshape(slots, 2, cols, row_total).astype(BF16)


def solution(mesh):
    placed = (P("wave", None, "tile", None), P("wave", None, None), P())
    return jax.shard_map(
        local, mesh=mesh, in_specs=placed, out_specs=P("wave", None, "tile", None), check_vma=False
    )
```

time: 188 us -> 98.3 us (0.52)
  other arithmetic: 77.2 us -> 20.9 us
  waiting for transfers between devices: 37.9 us -> 10.2 us
  between operations: 14.9 us -> 3 us
  blocking collectives: 20.8 us -> 10.7 us
  matrix products: 18.2 us -> 27.7 us
  starting transfers between devices: 6.35 us -> 13.4 us
    another operation x6 -> x8, other arithmetic: 64.8 us -> 1.38 us  [the longest x3 0.68 us: grid_products(): jnp.stack([energy, u * t, w * t, u * q]).reshape(grid_values.shape)]
    reduce_scatter x1 -> x0, waiting for transfers between devices: 37.9 us -> none  [local(): lax.psum_scatter(jnp.transpose(result, (1, 0, 2)), 'tile', scatter_dimens...]
    all_gather x1 -> x0, blocking collectives: 10.6 us -> none  [local(): shard_piece = lax.all_gather(fourier, 'tile', axis=4, tiled=True)]
    all_to_all x1 -> x3, waiting for transfers between devices: 0.01 us -> 10.2 us  [the longest x1 5.11 us: local(): lax.all_to_all(product, 'tile', split_axis=0, concat_axis=1, tiled=True)]
    dot_general x4 -> x12, matrix products: 18.2 us -> 27.7 us  [the longest x1 8.57 us: local(): lax.dot_general(masked, spec, (((2,), (2,)), ((0,), (0,))), preferred_ele...]
    cos x0 -> x2, other arithmetic: none -> 7.33 us  [trig(): return (jnp.cos(angles), jnp.sin(angles))]
    all_to_all x1 -> x3, starting transfers between devices: 6.35 us -> 13.4 us  [the longest x1 6.35 us: local(): lax.all_to_all(coefficients, 'wave', split_axis=0, concat_axis=3, tiled=T...]
    select_n x4 -> x10, other arithmetic: 2.57 us -> 6.69 us  [the longest x1 5.11 us: local(): jnp.where(upper, zero, legendre)]
  transfers between devices with their start and end apart: 2 -> 3, of which waited for: 1 -> 2; matrix products, arithmetic and copies ran while one was open for 34% -> 18% of each run, Pallas kernels for 0% -> 0%
where the time goes in v1:
time: 98.3 us; the launch traced here: 97.7 us
  matrix products  27.7 us (28%)
  other arithmetic  20.9 us (21%)
  starting transfers between devices  13.4 us (14%)
  local copies, waits for them, and re-layouts  11.9 us (12%)
  blocking collectives  10.7 us (11%)
  waiting for transfers between devices  10.2 us (10%)
  between operations  3 us (3%)
    all_to_all x1, blocking collectives, local(): lax.all_to_all(back, 'wave', split_axis=3, concat_axis=0, tiled=True)  10.7 us
    dot_general x1, matrix products, local(): lax.dot_general(masked, spec, (((2,), (2,)), ((0,), (0,))), preferred_ele...  8.57 us
    dot_general x1, matrix products, local(): lax.dot_general(returned, masked, (((2,), (1,)), ((0,), (0,))), preferred...  8.31 us
    cos x2, other arithmetic, trig(): return (jnp.cos(angles), jnp.sin(angles))  7.33 us
    all_to_all x1, starting transfers between devices, local(): lax.all_to_all(coefficients, 'wave', split_axis=0, concat_axis=3, tiled=T...  6.35 us
    all_to_all x1, waiting for transfers between devices, local(): lax.all_to_all(product, 'tile', split_axis=0, concat_axis=1, tiled=True)  5.11 us
    select_n x1, other arithmetic, local(): jnp.where(upper, zero, legendre)  5.11 us
    all_to_all x1, waiting for transfers between devices, local(): lax.all_to_all(grid_values, 'tile', split_axis=1, concat_axis=0, tiled=True)  5.08 us
  transfers between devices with their start and end apart: 3, of which 2 were waited for; matrix products, arithmetic and copies ran while one was open for 18% of the time, Pallas kernels for 0%

profile of v1, /device:TPU:0, one launch (start us, length us, event | category | flops | bytes accessed | tf_op | source)
XLA Modules:
  0.0 97.7 jit_solution(9886017591165895922)
XLA Ops:
  0.0 0.8 dynamic-slice_subtract_fusion
  0.8 0.2 iota_compare_fusion
  1.0 5.1 %broadcast_select_fusion.1 = (bf16[160,8,1281]{2,1,0:T(8,128)(2,1)}, bf16[160,8,1281]{2,1,0:T(8,128)(2,1)}) fusion(bf16[160,8,1281]{2,1,0:T(8,128)(2,1)} %param.4, pred[160,1281]{1,0:T(8,128)(4,1)S(1)} %iota_compare_fusion), kind=kLoop, calls=%fused_computation.10 | loop fusion | flops 3279360 | bytes 10043040 | tf_op jit(solution)/shard_map/jit(_where)/select_n | solution.py:74
  6.1 8.6 %fusion.12 = bf16[160,2,8,16]{3,2,1,0:T(8,128)(2,1)S(1)} fusion(bf16[160,2,8,1281]{3,2,1,0:T(8,128)(2,1)} %param.3, bf16[160,8,1281]{2,1,0:T(8,128)(2,1)} %get-tuple-element.27, bf16[160,8,1281]{2,1,0:T(8,128)(2,1)} %get-tuple-element.26), kind=kOutput, calls=%fused_computation.19 | convolution fusion | flops 118097920 | bytes 13199360 | tf_op jit(solution)/shard_map/dot_general | solution.py:98
  14.6 1.2 %copy.44 = bf16[160,2,8,16]{0,3,1,2:T(8,128)(2,1)} copy(bf16[160,2,8,16]{3,2,1,0:T(8,128)(2,1)S(1)} %fusion.12) | data formatting | bytes 163840 | tf_op jit(solution)/shard_map/reshape | solution.py:100
  15.9 6.3 %all-to-all-start = ((bf16[8,2,16,160]{3,2,1,0:T(8,128)(2,1)}), bf16[8,2,16,160]{3,2,1,0:T(8,128)(2,1)S(1)}, u32[]{:S(2)}, u32[]{:S(2)}) async-start(bf16[8,2,16,160]{3,2,1,0:T(8,128)(2,1)} %bitcast.5), calls=%async_computation | async-start | bytes 262144 | tf_op jit(solution)/shard_map/all_to_all | solution.py:102
  22.2 0.1 multiply_add_fusion.2
  22.3 0.1 rsqrt_multiply_fusion
  22.4 0.6 fusion.82
  25.6 1.3 %iota_compare_fusion.2 = (pred[1536]{0:T(1024)(128)(4,1)S(1)}, pred[1536]{0:T(1024)(128)(4,1)S(1)}) fusion(s32[]{:T(128)S(6)} %select_n.232, s32[]{:T(128)} %bitcast.2, s32[]{:T(128)} %bitcast.13), kind=kLoop, calls=%fused_computation.136 | loop fusion | flops 7680 | bytes 3084 | tf_op jit(solution)/shard_map/ge | solution.py:85
  26.9 1.3 %compare_select_fusion.1 = (s32[1536]{0:T(1024)S(1)}, f32[1536]{0:T(1024)S(1)}) fusion(s32[]{:T(128)} %bitcast.2, s32[]{:T(128)} %bitcast.13, s32[]{:T(128)S(6)} %select_n.232), kind=kLoop, calls=%fused_computation.123 | loop fusion | flops 7680 | bytes 12300 | tf_op jit(solution)/shard_map/jit(remainder)/jit(_where)/select_n | solution.py:32
  28.2 0.1 fusion.81
  28.3 2.1 %fusion.39 = (f32[20,1536]{1,0:T(8,128)S(1)}, f32[20,1536]{1,0:T(8,128)S(1)}) fusion(f32[1536]{0:T(1024)S(1)} %get-tuple-element.78, pred[1536]{0:T(1024)(128)(4,1)S(1)} %get-tuple-element.80, s32[1536]{0:T(1024)S(1)} %get-tuple-element.77, s32[1536]{0:T(1024)S(1)} %subtract_select_fusion, s32[20]{0:T(128)S(1)} %iota_multiply_fusion), kind=kLoop, calls=%fused_computation.65 | loop fusion | flops 337920 | bytes 265808 | tf_op jit(solution)/shard_map/cos | solution.py:34
  30.3 5.3 %fusion.27 = (f32[2,32,1536]{2,1,0:T(8,128)S(1)}, f32[2,32,1536]{2,1,0:T(8,128)S(1)}) fusion(f32[1536]{0:T(1024)S(1)} %get-tuple-element.78, pred[1536]{0:T(1024)(128)(4,1)S(1)} %get-tuple-element.80, s32[1536]{0:T(1024)S(1)} %get-tuple-element.77, s32[1536]{0:T(1024)S(1)} %subtract_select_fusion, s32[2,32]{1,0:T(2,128)S(1)} %multiply_add_fusion.1), kind=kLoop, calls=%fused_computation.40 | loop fusion | flops 1081344 | bytes 806656 | tf_op jit(solution)/shard_map/cos | solution.py:34
  35.6 2.5 %add_convert_fusion = (bf16[2,20,32,1536]{3,2,1,0:T(8,128)(2,1)S(1)}, bf16[2,20,32,1536]{3,2,1,0:T(8,128)(2,1)S(1)}) fusion(f32[2,32,1536]{2,1,0:T(8,128)S(1)} %get-tuple-element.62, f32[20,1536]{1,0:T(8,128)S(1)} %get-tuple-element.64, f32[2,32,1536]{2,1,0:T(8,128)S(1)} %get-tuple-element.61, f32[20,1536]{1,0:T(8,128)S(1)} %get-tuple-element.63), kind=kLoop, calls=%fused_computation | loop fusion | flops 15728640 | bytes 8896512 | tf_op jit(solution)/shard_map/convert_element_type | solution.py:46
  38.1 1.5 %fusion.75 = (bf16[1,20,32,1536]{3,2,1,0:T(8,128)(2,1)}, bf16[1,20,32,1536]{3,2,1,0:T(8,128)(2,1)S(1)}) fusion(bf16[2,20,32,1536]{3,2,1,0:T(8,128)(2,1)S(1)} %get-tuple-element.28), kind=kLoop, calls=%fused_computation.178 | loop fusion | bytes 7864320 | tf_op jit(solution)/shard_map/slice | solution.py:118
  39.6 2.3 %fusion.76 = (bf16[1,20,32,1536]{3,2,1,0:T(8,128)(2,1)}, bf16[1,20,32,1536]{3,2,1,0:T(8,128)(2,1)}) fusion(bf16[2,20,32,1536]{3,2,1,0:T(8,128)(2,1)S(1)} %get-tuple-element.29), kind=kLoop, calls=%fused_computation.179 | loop fusion | bytes 7864320 | tf_op jit(solution)/shard_map/slice | solution.py:118
  42.1 0.1 broadcast_compare_fusion
  42.2 0.1 mul.322
  42.2 0.1 stack.45
  42.3 0.1 stack.46
  42.4 0.1 copy.70
  42.5 0.1 all_to_all.45
  42.7 0.7 fusion.4
  43.4 0.2 reshape.906
  43.6 0.2 copy.68
  43.8 0.2 reshape.907
  44.0 2.1 %fusion.43 = f32[32,1536]{1,0:T(8,128)S(1)} fusion(bf16[640,1536]{1,0:T(8,128)(2,1)} %bitcast.174, bf16[16,640]{1,0:T(8,128)(2,1)S(1)} %get-tuple-element.43, bf16[16,640]{1,0:T(8,128)(2,1)S(1)} %get-tuple-element.49), kind=kOutput, calls=%fused_computation.92 | convolution fusion | flops 62996480 | bytes 2203648 | tf_op jit(solution)/shard_map/dot_general | solution.py:118
  46.1 2.0 %fusion.50 = f32[32,1536]{1,0:T(8,128)S(1)} fusion(bf16[640,1536]{1,0:T(8,128)(2,1)} %bitcast.170, bf16[16,640]{1,0:T(8,128)(2,1)S(1)} %get-tuple-element.47, bf16[16,640]{1,0:T(8,128)(2,1)S(1)} %get-tuple-element.50), kind=kOutput, calls=%fused_computation.99 | convolution fusion | flops 62996480 | bytes 2203648 | tf_op jit(solution)/shard_map/dot_general | solution.py:119
  48.1 0.5 convolution_add_fusion.1
  48.6 0.5 convolution_add_fusion
  49.1 0.7 pad_maximum_fusion.7
  49.8 3.7 %all-to-all-start.1 = ((bf16[8,8,768]{2,0,1:T(8,128)(2,1)}), bf16[8,8,768]{2,0,1:T(8,128)(2,1)S(1)}, u32[]{:S(2)}, u32[]{:S(2)}) async-start(bf16[8,8,768]{2,0,1:T(8,128)(2,1)} %bitcast.31), calls=%async_computation.1 | async-start | bytes 196608 | tf_op jit(solution)/shard_map/all_to_all | solution.py:126
  53.5 0.1 gt.16
  53.6 5.1 %all-to-all-done.1 = bf16[8,8,768]{2,0,1:T(8,128)(2,1)S(1)} async-done(((bf16[8,8,768]{2,0,1:T(8,128)(2,1)}), bf16[8,8,768]{2,0,1:T(8,128)(2,1)S(1)}, u32[]{:S(2)}, u32[]{:S(2)}) %all-to-all-start.1) | async-done | bytes 98336 | tf_op jit(solution)/shard_map/all_to_all | solution.py:126
  58.8 0.1 stack.96
  58.9 0.7 pad_maximum_fusion.8
  59.6 3.4 %all-to-all-start.2 = ((bf16[8,8,768]{2,1,0:T(8,128)(2,1)}), bf16[8,8,768]{2,1,0:T(8,128)(2,1)S(1)}, u32[]{:S(2)}, u32[]{:S(2)}) async-start(bf16[8,8,768]{2,1,0:T(8,128)(2,1)} %bitcast.40), calls=%async_computation.2 | async-start | bytes 196608 | tf_op jit(solution)/shard_map/all_to_all | solution.py:128
  62.9 5.1 %all-to-all-done.2 = bf16[8,8,768]{2,1,0:T(8,128)(2,1)S(1)} async-done(((bf16[8,8,768]{2,1,0:T(8,128)(2,1)}), bf16[8,8,768]{2,1,0:T(8,128)(2,1)S(1)}, u32[]{:S(2)}, u32[]{:S(2)}) %all-to-all-start.2) | async-done | bytes 98336 | tf_op jit(solution)/shard_map/all_to_all | solution.py:128
  68.2 2.3 %fusion.84 = f32[32,640]{1,0:T(8,128)S(1)} fusion(bf16[32,1536]{1,0:T(8,128)(2,1)S(1)} %bitcast.179, bf16[640,1536]{1,0:T(8,128)(2,1)} %bitcast.172), kind=kOutput, calls=%fused_computation.188 | convolution fusion | flops 62914560 | bytes 2146304 | tf_op jit(solution)/shard_map/dot_general | solution.py:139
  70.6 0.7 fusion.83
  71.2 0.7 fusion.86
  71.9 0.7 fusion.85
  72.7 0.1 squeeze.121
  72.8 0.1 squeeze.59
  72.9 0.1 squeeze.123
  73.0 0.1 squeeze.122
  73.1 0.1 squeeze.120
  73.2 0.1 squeeze.58
  73.3 0.1 neg.40
  73.4 0.1 squeeze.124
  73.6 0.1 fusion.37
  73.7 0.1 copy.53
  73.8 0.1 reshape.914
  73.9 0.7 fusion.15
  74.7 0.9 copy.54
  75.5 0.5 bitcast_bitcast_fusion
  76.0 0.7 reshape.950
  76.7 10.7 %all_to_all.56 = bf16[4,2,5120]{2,1,0:T(2,128)(2,1)S(1)} all-to-all(bf16[4,2,5120]{2,1,0:T(2,128)(2,1)S(1)} %reshape.950), channel_id=1, replica_groups=mesh['wave'=4,'tile'=8] {'wave'}, dimensions={0} | all-to-all | bytes 163840 | tf_op jit(solution)/shard_map/all_to_all | solution.py:157
  87.4 0.5 reshape.951
  87.8 0.9 copy.60
  88.8 0.1 copy.69
  88.9 0.5 copy.58
  89.4 8.3 %convert_bitcast_fusion = bf16[160,2,8,1281]{3,2,1,0:T(8,128)(2,1)} fusion(bf16[160,16,16]{2,1,0:T(8,128)(2,1)S(1)} %copy.58, bf16[160,8,1281]{2,1,0:T(8,128)(2,1)} %get-tuple-element.27, bf16[160,8,1281]{2,1,0:T(8,128)(2,1)} %get-tuple-element.26), kind=kOutput, calls=%fused_computation.5 | convolution fusion | flops 121336320 | bytes 13199360 | tf_op jit(solution)/shard_map/dot_general | solution.py:159
  (49 shorter events, 0.8 us)
Async XLA Ops:
  15.9 26.6 %all-to-all-start = ((bf16[8,2,16,160]{3,2,1,0:T(8,128)(2,1)}), bf16[8,2,16,160]{3,2,1,0:T(8,128)(2,1)S(1)}, u32[]{:S(2)}, u32[]{:S(2)}) async-start(bf16[8,2,16,160]{3,2,1,0:T(8,128)(2,1)} %bitcast.5), calls=%async_computation | async-start | bytes 262144 | tf_op jit(solution)/shard_map/all_to_all | solution.py:102
  39.6 3.0 %copy-start.3 = (s32[640]{0:T(1024)S(1)}, s32[640]{0:T(1024)}, u32[]{:S(2)}) copy-start(s32[640]{0:T(1024)} %param.5) | copy-start | bytes 7684
  43.9 4.2 %copy-start.1 = (bf16[1,20,32,1536]{3,2,1,0:T(8,128)(2,1)S(1)}, bf16[1,20,32,1536]{3,2,1,0:T(8,128)(2,1)}, u32[]{:S(2)}) copy-start(bf16[1,20,32,1536]{3,2,1,0:T(8,128)(2,1)} %get-tuple-element.22) | copy-start | bytes 5898244
  49.8 8.9 %all-to-all-start.1 = ((bf16[8,8,768]{2,0,1:T(8,128)(2,1)}), bf16[8,8,768]{2,0,1:T(8,128)(2,1)S(1)}, u32[]{:S(2)}, u32[]{:S(2)}) async-start(bf16[8,8,768]{2,0,1:T(8,128)(2,1)} %bitcast.31), calls=%async_computation.1 | async-start | bytes 196608 | tf_op jit(solution)/shard_map/all_to_all | solution.py:126
  59.6 8.5 %all-to-all-start.2 = ((bf16[8,8,768]{2,1,0:T(8,128)(2,1)}), bf16[8,8,768]{2,1,0:T(8,128)(2,1)S(1)}, u32[]{:S(2)}, u32[]{:S(2)}) async-start(bf16[8,8,768]{2,1,0:T(8,128)(2,1)} %bitcast.40), calls=%async_computation.2 | async-start | bytes 196608 | tf_op jit(solution)/shard_map/all_to_all | solution.py:128
  68.0 2.5 %copy-start.2 = (bf16[1,20,32,1536]{3,2,1,0:T(8,128)(2,1)S(1)}, bf16[1,20,32,1536]{3,2,1,0:T(8,128)(2,1)}, u32[]{:S(2)}) copy-start(bf16[1,20,32,1536]{3,2,1,0:T(8,128)(2,1)} %get-tuple-element.24) | copy-start | bytes 5898244
  68.1 3.8 %copy-start = (bf16[1,20,32,1536]{3,2,1,0:T(8,128)(2,1)S(1)}, bf16[1,20,32,1536]{3,2,1,0:T(8,128)(2,1)}, u32[]{:S(2)}) copy-start(bf16[1,20,32,1536]{3,2,1,0:T(8,128)(2,1)} %get-tuple-element.25) | copy-start | bytes 5898244

commit v2 on v1

v2 whole, which is shorter than its diff:
```python
import functools
import math

import jax
import jax.numpy as jnp
from jax import lax
from jax.experimental import pallas as pl
from jax.experimental.pallas import tpu as pltpu
from jax.sharding import PartitionSpec as P

MW = 1280
HALF_LATS = 1280
PAIRS = 640
NPTS = 5156
LANES = 128
RADIX = 32

F32 = jnp.float32
BF16 = jnp.bfloat16

HALF = MW // 2
GROUP = HALF // 2
GPAD = -(-GROUP // LANES) * LANES
BLOCKS = GPAD // RADIX
MESH = pl.DeviceIdType.MESH
NT = (((1,), (1,)), ((), ()))


def dot(a, b):
    return jnp.dot(a, b, preferred_element_type=F32)


def dot_nt(a, b):
    return lax.dot_general(a, b, NT, preferred_element_type=F32)


def middle_kernel(waves, tiles, cols, lat_count, kpad, *refs):
    (coef, ids, out, fx, gsend, grecv, psend, precv, bsend, cos_t, sin_t, small_c, small_s,
     hot, s1, r1, s2, r2, s3, r3, s4, r4) = refs
    wave, tile = lax.axis_index("wave"), lax.axis_index("tile")
    quarter = NPTS // 4
    halves = 4 * kpad // tiles
    per_d = tiles // 4
    rows = 2 * cols
    slots = coef.shape[2]

    def exchange(axis, here, count, src, dst, send, recv):
        copies = []
        for off in range(1, count):
            peer = lax.rem(here + off, count)
            copy = pltpu.make_async_remote_copy(
                src_ref=src.at[peer], dst_ref=dst.at[here], send_sem=send.at[off],
                recv_sem=recv.at[off], device_id={axis: peer}, device_id_type=MESH,
            )
            copy.start()
            copies.append(copy)
        dst[here] = src[here]
        return copies

    def finish(axis, here, count, src, dst, send, recv):
        for off in range(1, count):
            origin = lax.rem(here + count - off, count)
            pltpu.make_async_remote_copy(
                src_ref=src.at[origin], dst_ref=dst.at[origin], send_sem=send.at[off],
                recv_sem=recv.at[off], device_id={axis: origin}, device_id_type=MESH,
            ).wait_recv()

    barrier = pltpu.get_barrier_semaphore()
    for axis, here, count in (("wave", wave, waves), ("tile", tile, tiles)):
        for off in range(1, count):
            pl.semaphore_signal(
                barrier, inc=1, device_id={axis: lax.rem(here + off, count)}, device_id_type=MESH
            )
    pl.semaphore_wait(barrier, waves + tiles - 2)
    sends = exchange("wave", wave, waves, coef, fx, s1, r1)

    polar = wave * HALF // (lat_count // 2)
    q0 = 5 + polar
    n0, n1 = 4 * q0, NPTS - 4 * q0

    def line(shape, axis):
        return lax.broadcasted_iota(jnp.int32, shape, axis)

    k = line((1, kpad), 1)
    second = k >= q0
    inside = k < quarter
    point = jnp.where(inside, k - jnp.where(second, q0, 0), 0).astype(F32)
    length = jnp.where(second, n1, n0).astype(F32)

    def trig(m):
        whole = m.astype(F32) * point
        phase = whole - jnp.floor(whole / length) * length
        angle = (2.0 * math.pi) * phase / length
        return jnp.cos(angle), jnp.sin(angle)

    outer = 4 * BLOCKS
    r = line((outer, 1), 0)
    g, a = r // BLOCKS, r % BLOCKS
    c, s = trig((g // 2) * HALF + g % 2 + 2 * RADIX * a)
    small_c[0:outer] = c
    small_s[0:outer] = s
    c, s = trig(2 * line((RADIX, 1), 0))
    small_c[outer:] = c
    small_s[outer:] = s

    def block(idx, carry):
        ac, as_ = small_c[pl.ds(idx, 1), :], small_s[pl.ds(idx, 1), :]
        bc, bs = small_c[outer:, :], small_s[outer:, :]
        at = pl.ds(pl.multiple_of(idx * RADIX, RADIX), RADIX)
        cos_t[at, :] = (ac * bc - as_ * bs).astype(BF16)
        sin_t[at, :] = (as_ * bc + ac * bs).astype(BF16)
        return carry

    lax.fori_loop(0, outer, block, 0)

    lane = line((1, 2 * GPAD), 1)
    par = jnp.where(lane >= GPAD, 1, 0)
    i = lane - par * GPAD
    low = jnp.where(i < GROUP, 2 * i + par, -1)
    high = jnp.where(i < GROUP, HALF - 1 - par - 2 * i, -1)
    for w in range(waves):
        mine = ids[w]
        hot[0, w] = jnp.where(mine == low, 1.0, 0.0).astype(BF16)
        hot[1, w] = jnp.where(mine == high, 1.0, 0.0).astype(BF16)

    row = line((rows, 1), 0)
    n_row = jnp.where(row >= cols, n1, n0)
    cycle = jnp.where(row >= cols, HALF_LATS - 1 - polar, polar)
    weight = 40.0 * jnp.sin(math.pi * (cycle.astype(F32) + 0.5) / (2.0 * HALF_LATS))
    weight = weight / jnp.sqrt(lat_count * n_row.astype(F32))
    ii = line((1, GPAD), 1)
    up = ii % 2 == 0
    sign = jnp.where(up, 1.0, -1.0)

    def wavenumber(h, p):
        return h * HALF + p + 2 * ii

    def table(ref, h, p):
        start = (2 * h + p) * GPAD
        return ref[start : start + GPAD, :]

    finish("wave", wave, waves, coef, fx, s1, r1)
    even = jnp.zeros((2 * rows, kpad), F32)
    odd = jnp.zeros((2 * rows, kpad), F32)
    for h in range(2):
        both = jnp.zeros((2 * rows, 2 * GPAD), F32)
        for w in range(waves):
            both = both + dot(fx[w, h * 2 * rows : (h + 1) * 2 * rows, :], hot[h, w])
        for p in range(2):
            m = wavenumber(h, p)
            factor = jnp.where(2 * m < n_row, jnp.where(m == 0, 1.0, 2.0), 0.0)
            part = both[:, p * GPAD : (p + 1) * GPAD]
            re, im = part[:rows] * factor, part[rows:] * factor
            if p == 0:
                first = jnp.concatenate([re, re * sign]).astype(BF16)
                other = jnp.concatenate([-im, -im * sign]).astype(BF16)
                even = even + dot(first, table(cos_t, h, p)) + dot(other, table(sin_t, h, p))
            else:
                first = jnp.concatenate([re, im * sign]).astype(BF16)
                other = jnp.concatenate([-im, re * sign]).astype(BF16)
                odd = odd + dot(first, table(cos_t, h, p)) + dot(other, table(sin_t, h, p))

    def lat_of(x, v):
        return jnp.where(
            second, x[v * rows + cols : (v + 1) * rows], x[v * rows : v * rows + cols]
        )

    e0, e1, o0, o1 = lat_of(even, 0), lat_of(even, 1), lat_of(odd, 0), lat_of(odd, 1)
    for d, x in enumerate((e0 + o0, e1 - o1, e0 - o0, e1 + o1)):
        x = x.astype(BF16)
        for t in range(per_d):
            gsend[d * per_d + t] = x[:, t * halves : (t + 1) * halves]
    sends += exchange("tile", tile, tiles, gsend, grecv, s2, r2)
    finish("tile", tile, tiles, gsend, grecv, s2, r2)

    layers = cols * tiles // 4
    per_f = tiles // 4

    def field(f):
        return jnp.concatenate([grecv[f * per_f + t] for t in range(per_f)])

    u, w_, q = field(0).astype(F32), field(1).astype(F32), field(3).astype(F32)
    t16 = field(2)
    tri = jnp.where(line((layers, layers), 1) >= line((layers, layers), 0), 1.0, 0.0)
    geo = dot(tri.astype(BF16), t16) / math.sqrt(layers)
    temp = t16.astype(F32)
    for f, x in enumerate((0.5 * (u * u + w_ * w_) + geo, u * temp, w_ * temp, u * q)):
        x = x.astype(BF16)
        for t in range(per_f):
            psend[f * per_f + t] = x[t * cols : (t + 1) * cols]
    sends += exchange("tile", tile, tiles, psend, precv, s3, r3)
    finish("tile", tile, tiles, psend, precv, s3, r3)

    def quadrant(d):
        x = jnp.concatenate([precv[d * per_d + t].astype(F32) for t in range(per_d)], axis=1)
        return jnp.where(inside, x, 0.0)

    x0, x1, x2, x3 = [quadrant(d) for d in range(4)]

    def by_lat(*variants):
        return jnp.concatenate(
            [jnp.where(keep, v, 0.0) for v in variants for keep in (k < q0, second)]
        ).astype(BF16)

    even_in = by_lat((x0 + x2) + (x1 + x3), (x0 + x2) - (x1 + x3))
    odd_in = by_lat(x0 - x2, x1 - x3)
    for h in range(2):
        ec, es = dot_nt(even_in, table(cos_t, h, 0)), dot_nt(even_in, table(sin_t, h, 0))
        oc, os_ = dot_nt(odd_in, table(cos_t, h, 1)), dot_nt(odd_in, table(sin_t, h, 1))
        keep_e = jnp.where(2 * wavenumber(h, 0) < n_row, weight, 0.0)
        keep_o = jnp.where(2 * wavenumber(h, 1) < n_row, weight, 0.0)
        e_re = jnp.where(up, ec[:rows], ec[rows:]) * keep_e
        e_im = -jnp.where(up, es[:rows], es[rows:]) * keep_e
        o_re = (oc[:rows] - sign * os_[rows:]) * keep_o
        o_im = (-os_[:rows] - sign * oc[rows:]) * keep_o
        e_both = jnp.concatenate([e_re, e_im]).astype(BF16)
        o_both = jnp.concatenate([o_re, o_im]).astype(BF16)
        for w in range(waves):
            res = dot_nt(e_both, hot[h, w, :, :GPAD]) + dot_nt(o_both, hot[h, w, :, GPAD:])
            bsend[w, h * 2 * rows : (h + 1) * 2 * rows, :] = res.astype(BF16)
    sends += exchange("wave", wave, waves, bsend, out, s4, r4)
    finish("wave", wave, waves, bsend, out, s4, r4)
    for copy in sends:
        copy.wait_send()


def middle(coef, ids, waves, tiles, cols, lat_count):
    slots = coef.shape[2]
    step = max(tiles // 4, 1) * LANES
    kpad = -(-(NPTS // 4) // step) * step
    chunk = (tiles, cols, 4 * kpad // tiles)
    dma = pltpu.SemaphoreType.DMA
    vmem = pl.BlockSpec(memory_space=pltpu.VMEM)
    return pl.pallas_call(
        functools.partial(middle_kernel, waves, tiles, cols, lat_count, kpad),
        out_shape=jax.ShapeDtypeStruct(coef.shape, BF16),
        in_specs=[vmem, vmem],
        out_specs=vmem,
        scratch_shapes=[
            pltpu.VMEM(coef.shape, BF16),
            pltpu.VMEM(chunk, BF16), pltpu.VMEM(chunk, BF16),
            pltpu.VMEM(chunk, BF16), pltpu.VMEM(chunk, BF16),
            pltpu.VMEM(coef.shape, BF16),
            pltpu.VMEM((4 * GPAD, kpad), BF16), pltpu.VMEM((4 * GPAD, kpad), BF16),
            pltpu.VMEM((4 * BLOCKS + RADIX, kpad), F32),
            pltpu.VMEM((4 * BLOCKS + RADIX, kpad), F32),
            pltpu.VMEM((2, waves, slots, 2 * GPAD), BF16),
            dma((waves,)), dma((waves,)), dma((tiles,)), dma((tiles,)),
            dma((tiles,)), dma((tiles,)), dma((waves,)), dma((waves,)),
        ],
        compiler_params=pltpu.CompilerParams(
            collective_id=0, has_side_effects=True, vmem_limit_bytes=48 * 2**20
        ),
        name="middle",
    )(coef, ids)


def local(spectral, legendre, pair_ids):
    slots, _, cols, row_total = spectral.shape
    lat_count = legendre.shape[1]
    waves, tiles = lax.axis_size("wave"), lax.axis_size("tile")
    zero = jnp.zeros((), BF16)
    slot_ids = lax.dynamic_slice_in_dim(pair_ids, lax.axis_index("wave") * slots, slots)
    row_index = lax.broadcasted_iota(jnp.int32, (slots, row_total), 1)
    upper = (row_index >= (MW - slot_ids)[:, None])[:, None, :]
    masked = jnp.concatenate(
        [jnp.where(upper, zero, legendre), jnp.where(upper, legendre, zero)], axis=1
    )
    spec = spectral.reshape(slots, 2 * cols, row_total)
    coef = lax.dot_general(
        masked, spec, (((2,), (2,)), ((0,), (0,))), preferred_element_type=F32
    ).astype(BF16)
    coef = coef.reshape(slots, 2, waves, 2, 2, cols).transpose(2, 1, 4, 3, 5, 0)
    coef = coef.reshape(waves, 8 * cols, slots)
    back = middle(coef, pair_ids.reshape(waves, slots, 1), waves, tiles, cols, lat_count)
    back = back.reshape(waves, 2, 2, 2, cols, slots).transpose(5, 2, 4, 1, 0, 3)
    back = back.reshape(slots, 2 * cols, 2 * lat_count)
    result = lax.dot_general(
        back, masked, (((2,), (1,)), ((0,), (0,))), preferred_element_type=F32
    )
    return result.reshape(slots, 2, cols, row_total).astype(BF16)


def solution(mesh):
    placed = (P("wave", None, "tile", None), P("wave", None, None), P())
    return jax.shard_map(
        local, mesh=mesh, in_specs=placed, out_specs=P("wave", None, "tile", None), check_vma=False
    )
```

time: 98.3 us -> 53.5 us (0.54)
  Pallas kernels: 0 us -> 28.2 us
  other arithmetic: 20.9 us -> 6.07 us
  starting transfers between devices: 13.4 us -> 0 us
  matrix products: 27.7 us -> 16.9 us
  blocking collectives: 10.7 us -> 0 us
  waiting for transfers between devices: 10.2 us -> 0 us
  local copies, waits for them, and re-layouts: 11.9 us -> 2.07 us
  between operations: 3 us -> 0.05 us
    pallas_call x0 -> x1, Pallas kernels: none -> 28.2 us  [middle(): pl.pallas_call(functools.partial(middle_kernel, waves, tiles, cols, lat_c...]
    all_to_all x3 -> x0, starting transfers between devices: 13.4 us -> none  [the longest x1 6.35 us: local(): lax.all_to_all(coefficients, 'wave', split_axis=0, concat_axis=3, tiled=T...]
    dot_general x11 -> x1, matrix products: 19.1 us -> 8.31 us  [local(): lax.dot_general(back, masked, (((2,), (1,)), ((0,), (0,))), preferred_ele...]
    all_to_all x1 -> x0, blocking collectives: 10.7 us -> none  [local(): lax.all_to_all(back, 'wave', split_axis=3, concat_axis=0, tiled=True)]
    all_to_all x3 -> x0, waiting for transfers between devices: 10.2 us -> none  [the longest x1 5.11 us: local(): lax.all_to_all(product, 'tile', split_axis=0, concat_axis=1, tiled=True)]
    cos x2 -> x0, other arithmetic: 7.33 us -> none  [trig(): return (jnp.cos(angles), jnp.sin(angles))]
    slice x7 -> x0, local copies, waits for them, and re-layouts: 4.44 us -> none  [the longest x2 3.79 us: local(): even = (dot(even_c, cos[0]) + dot(even_s, sin[0])).reshape(2, 2, cols, kpad)]
    convert_element_type x4 -> x0, other arithmetic: 2.57 us -> none  [the longest x1 2.49 us: tables(): sin = (a_sin * b_cos + a_cos * b_sin).astype(BF16).reshape(2, MW // 2, pts)]
  transfers between devices with their start and end apart: 3 -> 0, of which waited for: 2 -> 0; matrix products, arithmetic and copies ran while one was open for 18% -> 0% of each run, Pallas kernels for 0% -> 0%
where the time goes in v2:
time: 53.5 us; the launch traced here: 53.3 us
  Pallas kernels  28.2 us (53%)
  matrix products  16.9 us (32%)
  other arithmetic  6.07 us (11%)
  local copies, waits for them, and re-layouts  2.07 us (4%)
    pallas_call x1, Pallas kernels, middle(): pl.pallas_call(functools.partial(middle_kernel, waves, tiles, cols, lat_c...  28.2 us
    dot_general x1, matrix products, local(): lax.dot_general(masked, spec, (((2,), (2,)), ((0,), (0,))), preferred_ele...  8.57 us
    dot_general x1, matrix products, local(): lax.dot_general(back, masked, (((2,), (1,)), ((0,), (0,))), preferred_ele...  8.31 us
    select_n x1, other arithmetic, local(): jnp.where(upper, zero, legendre)  5.12 us

profile of v2, /device:TPU:0, one launch (start us, length us, event | category | flops | bytes accessed | tf_op | source)
XLA Modules:
  0.0 53.3 jit_solution(11684730216776046493)
XLA Ops:
  0.0 0.8 %dynamic-slice_subtract_fusion = s32[160]{0:T(256)S(1)} fusion(s32[640]{0:T(1024)} %param.5, s32[]{:T(128)S(6)} %select_n.11), kind=kLoop, calls=%fused_computation.8 | loop fusion | flops 160 | bytes 1284 | tf_op jit(solution)/shard_map/sub | solution.py:265
  0.8 0.2 iota_compare_fusion
  1.0 0.9 %reshape.41.refs_1_ = s32[4,160,1]{2,1,0:T(8,128)S(1)} reshape(s32[640]{0:T(1024)} %param.5) | data formatting | bytes 5120 | tf_op jit(solution)/shard_map/reshape | solution.py:275
  1.9 5.1 %broadcast_select_fusion.1 = (bf16[160,8,1281]{2,1,0:T(8,128)(2,1)}, bf16[160,8,1281]{2,1,0:T(8,128)(2,1)}) fusion(bf16[160,8,1281]{2,1,0:T(8,128)(2,1)} %param.4, pred[160,1281]{1,0:T(8,128)(4,1)S(1)} %iota_compare_fusion), kind=kLoop, calls=%fused_computation.5 | loop fusion | flops 3279360 | bytes 10043040 | tf_op jit(solution)/shard_map/jit(_where)/select_n | solution.py:267
  7.0 8.6 %fusion.2 = bf16[160,16,16]{2,1,0:T(8,128)(2,1)S(1)} fusion(bf16[160,2,8,1281]{3,2,1,0:T(8,128)(2,1)} %param.3, bf16[160,8,1281]{2,1,0:T(8,128)(2,1)} %get-tuple-element.6, bf16[160,8,1281]{2,1,0:T(8,128)(2,1)} %get-tuple-element.5), kind=kOutput, calls=%fused_computation.6 | convolution fusion | flops 118097920 | bytes 13199360 | tf_op jit(solution)/shard_map/dot_general | solution.py:270
  15.6 0.6 %copy.6 = bf16[160,16,16]{0,2,1:T(8,128)(2,1)S(1)} copy(bf16[160,16,16]{2,1,0:T(8,128)(2,1)S(1)} %fusion.2) | data formatting | bytes 163840 | tf_op jit(solution)/shard_map/convert_element_type | solution.py:272
  16.1 28.2 %middle.1 = bf16[4,64,160]{2,1,0:T(8,128)(2,1)S(1)} custom-call(bf16[4,64,160]{2,1,0:T(8,128)(2,1)S(1)} %bitcast.16, s32[4,160,1]{2,1,0:T(8,128)S(1)} %reshape.41.refs_1_), custom_call_target="tpu_custom_call" | custom-call | tf_op jit(solution)/shard_map/middle/pallas_call | solution.py:234
  44.4 0.6 %copy.10 = bf16[160,16,16]{2,1,0:T(8,128)(2,1)S(1)} copy(bf16[160,16,16]{0,1,2:T(8,128)(2,1)S(1)} %bitcast.19) | data formatting | bytes 163840 | tf_op jit(solution)/shard_map/reshape | solution.py:277
  45.0 8.3 %convert_bitcast_fusion = bf16[160,2,8,1281]{3,2,1,0:T(8,128)(2,1)} fusion(bf16[160,16,16]{2,1,0:T(8,128)(2,1)S(1)} %copy.10, bf16[160,8,1281]{2,1,0:T(8,128)(2,1)} %get-tuple-element.6, bf16[160,8,1281]{2,1,0:T(8,128)(2,1)} %get-tuple-element.5), kind=kOutput, calls=%fused_computation.3 | convolution fusion | flops 121336320 | bytes 13199360 | tf_op jit(solution)/shard_map/dot_general | solution.py:278
  (2 shorter events, 0.0 us)

commit v3 on v2

--- a/solution.py
+++ b/solution.py
@@ -113,15 +113,13 @@
 
     lax.fori_loop(0, outer, block, 0)
 
-    lane = line((1, 2 * GPAD), 1)
+    lane = line((2 * GPAD, 1), 0)
     par = jnp.where(lane >= GPAD, 1, 0)
     i = lane - par * GPAD
     low = jnp.where(i < GROUP, 2 * i + par, -1)
     high = jnp.where(i < GROUP, HALF - 1 - par - 2 * i, -1)
-    for w in range(waves):
-        mine = ids[w]
-        hot[0, w] = jnp.where(mine == low, 1.0, 0.0).astype(BF16)
-        hot[1, w] = jnp.where(mine == high, 1.0, 0.0).astype(BF16)
+    hot[0] = jnp.where(ids[...] == low, 1.0, 0.0).astype(BF16)
+    hot[1] = jnp.where(ids[...] == high, 1.0, 0.0).astype(BF16)
 
     row = line((rows, 1), 0)
     n_row = jnp.where(row >= cols, n1, n0)
@@ -143,9 +141,8 @@
     even = jnp.zeros((2 * rows, kpad), F32)
     odd = jnp.zeros((2 * rows, kpad), F32)
     for h in range(2):
-        both = jnp.zeros((2 * rows, 2 * GPAD), F32)
-        for w in range(waves):
-            both = both + dot(fx[w, h * 2 * rows : (h + 1) * 2 * rows, :], hot[h, w])
+        here = [fx[w, h * 2 * rows : (h + 1) * 2 * rows, :] for w in range(waves)]
+        both = dot_nt(jnp.concatenate(here, axis=1), hot[h])
         for p in range(2):
             m = wavenumber(h, p)
             factor = jnp.where(2 * m < n_row, jnp.where(m == 0, 1.0, 2.0), 0.0)
@@ -215,9 +212,9 @@
         o_im = (-os_[:rows] - sign * oc[rows:]) * keep_o
         e_both = jnp.concatenate([e_re, e_im]).astype(BF16)
         o_both = jnp.concatenate([o_re, o_im]).astype(BF16)
+        res = (dot(e_both, hot[h, :GPAD]) + dot(o_both, hot[h, GPAD:])).astype(BF16)
         for w in range(waves):
-            res = dot_nt(e_both, hot[h, w, :, :GPAD]) + dot_nt(o_both, hot[h, w, :, GPAD:])
-            bsend[w, h * 2 * rows : (h + 1) * 2 * rows, :] = res.astype(BF16)
+            bsend[w, h * 2 * rows : (h + 1) * 2 * rows, :] = res[:, w * slots : (w + 1) * slots]
     sends += exchange("wave", wave, waves, bsend, out, s4, r4)
     finish("wave", wave, waves, bsend, out, s4, r4)
     for copy in sends:
@@ -244,7 +241,7 @@
             pltpu.VMEM((4 * GPAD, kpad), BF16), pltpu.VMEM((4 * GPAD, kpad), BF16),
             pltpu.VMEM((4 * BLOCKS + RADIX, kpad), F32),
             pltpu.VMEM((4 * BLOCKS + RADIX, kpad), F32),
-            pltpu.VMEM((2, waves, slots, 2 * GPAD), BF16),
+            pltpu.VMEM((2, 2 * GPAD, waves * slots), BF16),
             dma((waves,)), dma((waves,)), dma((tiles,)), dma((tiles,)),
             dma((tiles,)), dma((tiles,)), dma((waves,)), dma((waves,)),
         ],
@@ -255,30 +252,86 @@
     )(coef, ids)
 
 
+def halves_of(ids, legendre, base, lane):
+    parts = []
+    for b in range(legendre.shape[0]):
+        block = legendre[b]
+        low = jnp.where(lane < MW - ids[base + b], 1.0, 0.0).astype(BF16) * block
+        parts += [low, block - low]
+    return jnp.concatenate(parts)
+
+
+def same_slot(shape, rows, columns):
+    row = lax.broadcasted_iota(jnp.int32, shape, 0) // rows
+    return row == lax.broadcasted_iota(jnp.int32, shape, 1) // columns
+
+
+def fold(rows, columns):
+    row = lax.broadcasted_iota(jnp.int32, (rows, columns), 0) % columns
+    same = row == lax.broadcasted_iota(jnp.int32, (rows, columns), 1)
+    return jnp.where(same, 1.0, 0.0).astype(BF16)
+
+
+def forward_kernel(slots, ids, spectral, legendre, out):
+    take, lats, row_total = legendre.shape
+    fields = spectral.shape[1] * spectral.shape[2]
+    base = lax.axis_index("wave") * slots + pl.program_id(0) * take
+    lane = lax.broadcasted_iota(jnp.int32, (1, row_total), 1)
+    left = halves_of(ids, legendre, base, lane)
+    right = spectral[...].reshape(take * fields, row_total)
+    full = dot_nt(left, right)
+    full = jnp.where(same_slot(full.shape, 2 * lats, fields), full, 0.0).astype(BF16)
+    out[0] = dot(full, fold(take * fields, fields)).astype(BF16)
+
+
+def inverse_kernel(slots, ids, back, legendre, out):
+    take, lats, row_total = legendre.shape
+    fields = out.shape[1] * out.shape[2]
+    base = lax.axis_index("wave") * slots + pl.program_id(0) * take
+    lane = lax.broadcasted_iota(jnp.int32, (1, row_total), 1)
+    right = halves_of(ids, legendre, base, lane)
+    wide = dot_nt(back[0], fold(take * 2 * lats, 2 * lats))
+    wide = jnp.where(same_slot(wide.shape, fields, 2 * lats), wide, 0.0).astype(BF16)
+    out[...] = dot(wide, right).astype(BF16).reshape(out.shape)
+
+
 def local(spectral, legendre, pair_ids):
     slots, _, cols, row_total = spectral.shape
     lat_count = legendre.shape[1]
     waves, tiles = lax.axis_size("wave"), lax.axis_size("tile")
-    zero = jnp.zeros((), BF16)
-    slot_ids = lax.dynamic_slice_in_dim(pair_ids, lax.axis_index("wave") * slots, slots)
-    row_index = lax.broadcasted_iota(jnp.int32, (slots, row_total), 1)
-    upper = (row_index >= (MW - slot_ids)[:, None])[:, None, :]
-    masked = jnp.concatenate(
-        [jnp.where(upper, zero, legendre), jnp.where(upper, legendre, zero)], axis=1
-    )
-    spec = spectral.reshape(slots, 2 * cols, row_total)
-    coef = lax.dot_general(
-        masked, spec, (((2,), (2,)), ((0,), (0,))), preferred_element_type=F32
-    ).astype(BF16)
+    take = max(b for b in range(1, 17) if slots % b == 0)
+    groups = slots // take
+    smem = pl.BlockSpec(memory_space=pltpu.SMEM)
+    spec_block = pl.BlockSpec((take, 2, cols, row_total), lambda g: (g, 0, 0, 0))
+    leg_block = pl.BlockSpec((take, lat_count, row_total), lambda g: (g, 0, 0))
+    params = pltpu.CompilerParams(vmem_limit_bytes=40 * 2**20)
+    coef = pl.pallas_call(
+        functools.partial(forward_kernel, slots),
+        grid=(groups,),
+        out_shape=jax.ShapeDtypeStruct((groups, take * 2 * lat_count, 2 * cols), BF16),
+        in_specs=[smem, spec_block, leg_block],
+        out_specs=pl.BlockSpec((1, take * 2 * lat_count, 2 * cols), lambda g: (g, 0, 0)),
+        compiler_params=params,
+        name="forward",
+    )(pair_ids, spectral, legendre)
     coef = coef.reshape(slots, 2, waves, 2, 2, cols).transpose(2, 1, 4, 3, 5, 0)
     coef = coef.reshape(waves, 8 * cols, slots)
-    back = middle(coef, pair_ids.reshape(waves, slots, 1), waves, tiles, cols, lat_count)
+    back = middle(coef, pair_ids.reshape(1, PAIRS), waves, tiles, cols, lat_count)
     back = back.reshape(waves, 2, 2, 2, cols, slots).transpose(5, 2, 4, 1, 0, 3)
-    back = back.reshape(slots, 2 * cols, 2 * lat_count)
-    result = lax.dot_general(
-        back, masked, (((2,), (1,)), ((0,), (0,))), preferred_element_type=F32
-    )
-    return result.reshape(slots, 2, cols, row_total).astype(BF16)
+    back = back.reshape(groups, take * 2 * cols, 2 * lat_count)
+    return pl.pallas_call(
+        functools.partial(inverse_kernel, slots),
+        grid=(groups,),
+        out_shape=jax.ShapeDtypeStruct(spectral.shape, BF16),
+        in_specs=[
+            smem,
+            pl.BlockSpec((1, take * 2 * cols, 2 * lat_count), lambda g: (g, 0, 0)),
+            leg_block,
+        ],
+        out_specs=spec_block,
+        compiler_params=params,
+        name="inverse",
+    )(pair_ids, back, legendre)
 
 
 def solution(mesh):

time: 53.5 us -> 55.9 us (1.045)
  matrix products: 16.9 us -> 0 us
  Pallas kernels: 28.2 us -> 41.9 us
  local copies, waits for them, and re-layouts: 2.07 us -> 13.7 us
  other arithmetic: 6.07 us -> 0 us
    dot_general x2 -> x0, matrix products: 16.9 us -> none  [the longest x1 8.57 us: local(): lax.dot_general(masked, spec, (((2,), (2,)), ((0,), (0,))), preferred_ele...]
    pallas_call x0 -> x2, Pallas kernels: none -> 14.6 us  [the longest x1 8.11 us: local(): pl.pallas_call(functools.partial(inverse_kernel, slots), grid=(groups,),...]
    unnamed x0 -> x10, local copies, waits for them, and re-layouts: none -> 7.77 us
    select_n x1 -> x0, other arithmetic: 5.12 us -> none  [local(): jnp.where(upper, zero, legendre)]
    reshape x2 -> x4, local copies, waits for them, and re-layouts: 1.5 us -> 3.69 us  [the longest x2 2.52 us: local(): back = back.reshape(groups, take * 2 * cols, 2 * lat_count)]
    transpose x1, local copies, waits for them, and re-layouts: 0.01 us -> 1.28 us  [local(): coef = coef.reshape(slots, 2, waves, 2, 2, cols).transpose(2, 1, 4, 3, 5, 0)]
    reshape x1, local copies, waits for them, and re-layouts: 0.01 us -> 0.99 us  [local(): back = back.reshape(waves, 2, 2, 2, cols, slots).transpose(5, 2, 4, 1, 0, 3)]
    pallas_call x1, Pallas kernels: 28.2 us -> 27.3 us  [middle(): pl.pallas_call(functools.partial(middle_kernel, waves, tiles, cols, lat_c...]
where the time goes in v3:
time: 55.9 us; the launch traced here: 55.7 us
  Pallas kernels  41.9 us (75%)
  local copies, waits for them, and re-layouts  13.7 us (25%)
    pallas_call x1, Pallas kernels, middle(): pl.pallas_call(functools.partial(middle_kernel, waves, tiles, cols, lat_c...  27.3 us
    pallas_call x1, Pallas kernels, local(): pl.pallas_call(functools.partial(inverse_kernel, slots), grid=(groups,),...  8.11 us
    unnamed x10, local copies, waits for them, and re-layouts  7.77 us
    pallas_call x1, Pallas kernels, local(): pl.pallas_call(functools.partial(forward_kernel, slots), grid=(groups,),...  6.47 us
    reshape x2, local copies, waits for them, and re-layouts, local(): back = back.reshape(groups, take * 2 * cols, 2 * lat_count)  2.52 us
    transpose x1, local copies, waits for them, and re-layouts, local(): coef = coef.reshape(slots, 2, waves, 2, 2, cols).transpose(2, 1, 4, 3, 5, 0)  1.28 us

profile of v3, /device:TPU:0, one launch (start us, length us, event | category | flops | bytes accessed | tf_op | source)
XLA Modules:
  0.0 55.7 jit_solution(7162144238978844215)
XLA Ops:
  0.0 0.7 %reshape.17.refs_1_ = s32[1,640]{1,0:T(1,128)S(1)} reshape(s32[640]{0:T(1024)} %ids.3) | data formatting | bytes 5120 | tf_op jit(solution)/shard_map/reshape | solution.py:319
  0.7 0.0 copy-start
  0.7 2.0 %copy-done = bf16[160,8,1281]{2,1,0:T(8,128)(2,1)S(1)} copy-done((bf16[160,8,1281]{2,1,0:T(8,128)(2,1)S(1)}, bf16[160,8,1281]{2,1,0:T(8,128)(2,1)}, u32[]{:S(2)}) %copy-start) | copy-done | bytes 3279384
  2.7 0.0 copy-start.2
  2.7 3.0 %copy-done.2 = bf16[160,2,8,1281]{3,2,1,0:T(8,128)(2,1)S(1)} copy-done((bf16[160,2,8,1281]{3,2,1,0:T(8,128)(2,1)S(1)}, bf16[160,2,8,1281]{3,2,1,0:T(8,128)(2,1)}, u32[]{:S(2)}) %copy-start.2) | copy-done | bytes 6558744
  5.8 0.0 copy-start.3
  5.8 0.7 %copy-done.3 = s32[640]{0:T(1024)S(1)} copy-done((s32[640]{0:T(1024)S(1)}, s32[640]{0:T(1024)}, u32[]{:S(2)}) %copy-start.3) | copy-done | bytes 2584
  6.4 6.5 %forward.1 = bf16[10,256,16]{2,1,0:T(8,128)(2,1)S(1)} custom-call(s32[640]{0:T(1024)S(1)} %copy-done.3, bf16[160,2,8,1281]{3,2,1,0:T(8,128)(2,1)S(1)} %copy-done.2, bf16[160,8,1281]{2,1,0:T(8,128)(2,1)S(1)} %copy-done), custom_call_target="tpu_custom_call" | custom-call | tf_op jit(solution)/shard_map/forward/pallas_call | solution.py:308
  12.9 0.0 copy-start.4
  12.9 0.5 reshape.15
  13.4 1.3 %copy.6 = bf16[4,2,2,2,8,160]{5,4,3,2,1,0:T(8,128)(2,1)S(1)} copy(bf16[4,2,2,2,8,160]{4,2,3,0,1,5:T(2,128)(2,1)S(1)} %bitcast.8) | data formatting | bytes 163840 | tf_op jit(solution)/shard_map/transpose | solution.py:317
  14.7 27.3 %middle.1 = bf16[4,64,160]{2,1,0:T(8,128)(2,1)S(1)} custom-call(bf16[4,64,160]{2,1,0:T(8,128)(2,1)S(1)} %bitcast.6, s32[1,640]{1,0:T(1,128)S(1)} %reshape.17.refs_1_), custom_call_target="tpu_custom_call" | custom-call | tf_op jit(solution)/shard_map/middle/pallas_call | solution.py:231
  42.0 1.0 %copy.7 = bf16[4,2,2,2,8,160]{4,2,5,3,0,1:T(2,128)(2,1)S(1)} copy(bf16[4,2,2,2,8,160]{5,4,3,2,1,0:T(8,128)(2,1)S(1)} %bitcast.7) | data formatting | bytes 163840 | tf_op jit(solution)/shard_map/reshape | solution.py:320
  43.0 2.2 %reshape.19 = bf16[10,256,16]{1,0,2:T(8,128)(2,1)S(1)} reshape(bf16[160,2,8,2,4,2]{2,1,0,5,4,3:T(2,128)(2,1)S(1)} %bitcast.9) | data formatting | bytes 163840 | tf_op jit(solution)/shard_map/reshape | solution.py:321
  45.2 0.3 copy.8.back
  45.5 0.0 copy-done.4
  45.5 0.0 copy-start.1
  45.5 2.0 %copy-done.1 = bf16[160,8,1281]{2,1,0:T(8,128)(2,1)S(1)} copy-done((bf16[160,8,1281]{2,1,0:T(8,128)(2,1)S(1)}, bf16[160,8,1281]{2,1,0:T(8,128)(2,1)}, u32[]{:S(2)}) %copy-start.1) | copy-done | bytes 3279384
  47.6 8.1 %inverse.1 = bf16[160,2,8,1281]{3,2,1,0:T(8,128)(2,1)} custom-call(s32[640]{0:T(1024)S(1)} %copy-done.4, bf16[10,256,16]{2,1,0:T(8,128)(2,1)S(1)} %copy.8.back, bf16[160,8,1281]{2,1,0:T(8,128)(2,1)S(1)} %copy-done.1), custom_call_target="tpu_custom_call" | custom-call | tf_op jit(solution)/shard_map/inverse/pallas_call | solution.py:322
Async XLA Ops:
  0.7 2.0 %copy-start = (bf16[160,8,1281]{2,1,0:T(8,128)(2,1)S(1)}, bf16[160,8,1281]{2,1,0:T(8,128)(2,1)}, u32[]{:S(2)}) copy-start(bf16[160,8,1281]{2,1,0:T(8,128)(2,1)} %legendre.3) | copy-start | bytes 9838084
  2.7 3.0 %copy-start.2 = (bf16[160,2,8,1281]{3,2,1,0:T(8,128)(2,1)S(1)}, bf16[160,2,8,1281]{3,2,1,0:T(8,128)(2,1)}, u32[]{:S(2)}) copy-start(bf16[160,2,8,1281]{3,2,1,0:T(8,128)(2,1)} %spectral.1) | copy-start | bytes 19676164
  5.8 0.7 %copy-start.3 = (s32[640]{0:T(1024)S(1)}, s32[640]{0:T(1024)}, u32[]{:S(2)}) copy-start(s32[640]{0:T(1024)} %ids.3) | copy-start | bytes 7684
  12.9 32.6 %copy-start.4 = (s32[640]{0:T(1024)S(1)}, s32[640]{0:T(1024)}, u32[]{:S(2)}) copy-start(s32[640]{0:T(1024)} %ids.3) | copy-start | bytes 7684
  45.5 2.0 %copy-start.1 = (bf16[160,8,1281]{2,1,0:T(8,128)(2,1)S(1)}, bf16[160,8,1281]{2,1,0:T(8,128)(2,1)}, u32[]{:S(2)}) copy-start(bf16[160,8,1281]{2,1,0:T(8,128)(2,1)} %legendre.3) | copy-start | bytes 9838084

commit v4 on v3

--- a/solution.py
+++ b/solution.py
@@ -22,6 +22,7 @@
 GROUP = HALF // 2
 GPAD = -(-GROUP // LANES) * LANES
 BLOCKS = GPAD // RADIX
+SPAN = 16
 MESH = pl.DeviceIdType.MESH
 NT = (((1,), (1,)), ((), ()))
 
@@ -35,8 +36,8 @@
 
 
 def middle_kernel(waves, tiles, cols, lat_count, kpad, *refs):
-    (coef, ids, out, fx, gsend, grecv, psend, precv, bsend, cos_t, sin_t, small_c, small_s,
-     hot, s1, r1, s2, r2, s3, r3, s4, r4) = refs
+    (coef, ids, out, fx, gsend, grecv, psend, precv, bsend, trig_t, small_c, small_s, hot,
+     s1, r1, s2, r2, s3, r3, s4, r4) = refs
     wave, tile = lax.axis_index("wave"), lax.axis_index("tile")
     quarter = NPTS // 4
     halves = 4 * kpad // tiles
@@ -93,33 +94,42 @@
         angle = (2.0 * math.pi) * phase / length
         return jnp.cos(angle), jnp.sin(angle)
 
-    outer = 4 * BLOCKS
-    r = line((outer, 1), 0)
-    g, a = r // BLOCKS, r % BLOCKS
-    c, s = trig((g // 2) * HALF + g % 2 + 2 * RADIX * a)
-    small_c[0:outer] = c
-    small_s[0:outer] = s
-    c, s = trig(2 * line((RADIX, 1), 0))
-    small_c[outer:] = c
-    small_s[outer:] = s
+    r = line((RADIX, 1), 0)
+    m = jnp.where(r < 8, 2 * r, 16 * (r - 8))
+    m = jnp.where(r >= 12, (r - 12) // 2 * HALF + (r - 12) % 2, m)
+    m = jnp.where(r >= 16, 2 * RADIX * (r - 16), m)
+    c, s = trig(m)
+    outer = 4 * SPAN
+    for g in range(4):
+        ca, sa, cb, sb = c[16:], s[16:], c[12 + g : 13 + g], s[12 + g : 13 + g]
+        small_c[g * SPAN : (g + 1) * SPAN] = ca * cb - sa * sb
+        small_s[g * SPAN : (g + 1) * SPAN] = sa * cb + ca * sb
+        ca, sa, cb, sb = c[:8], s[:8], c[8 + g : 9 + g], s[8 + g : 9 + g]
+        small_c[outer + 8 * g : outer + 8 * g + 8] = ca * cb - sa * sb
+        small_s[outer + 8 * g : outer + 8 * g + 8] = sa * cb + ca * sb
 
     def block(idx, carry):
-        ac, as_ = small_c[pl.ds(idx, 1), :], small_s[pl.ds(idx, 1), :]
+        g, a = idx // BLOCKS, idx % BLOCKS
+        row_a = g * SPAN + a
+        ac, as_ = small_c[pl.ds(row_a, 1), :], small_s[pl.ds(row_a, 1), :]
         bc, bs = small_c[outer:, :], small_s[outer:, :]
-        at = pl.ds(pl.multiple_of(idx * RADIX, RADIX), RADIX)
-        cos_t[at, :] = (ac * bc - as_ * bs).astype(BF16)
-        sin_t[at, :] = (as_ * bc + ac * bs).astype(BF16)
+        at = ((g % 2) * 4 + g // 2) * GPAD + a * RADIX
+        cos_at = pl.ds(pl.multiple_of(at, RADIX), RADIX)
+        sin_at = pl.ds(pl.multiple_of(at + 2 * GPAD, RADIX), RADIX)
+        trig_t[cos_at, :] = (ac * bc - as_ * bs).astype(BF16)
+        trig_t[sin_at, :] = (as_ * bc + ac * bs).astype(BF16)
         return carry
 
-    lax.fori_loop(0, outer, block, 0)
+    lax.fori_loop(0, 4 * BLOCKS, block, 0)
 
     lane = line((2 * GPAD, 1), 0)
     par = jnp.where(lane >= GPAD, 1, 0)
     i = lane - par * GPAD
     low = jnp.where(i < GROUP, 2 * i + par, -1)
     high = jnp.where(i < GROUP, HALF - 1 - par - 2 * i, -1)
-    hot[0] = jnp.where(ids[...] == low, 1.0, 0.0).astype(BF16)
-    hot[1] = jnp.where(ids[...] == high, 1.0, 0.0).astype(BF16)
+    pair = ids[...].reshape(1, ids.shape[0])
+    hot[0] = jnp.where(pair == low, 1.0, 0.0).astype(BF16)
+    hot[1] = jnp.where(pair == high, 1.0, 0.0).astype(BF16)
 
     row = line((rows, 1), 0)
     n_row = jnp.where(row >= cols, n1, n0)
@@ -133,13 +143,11 @@
     def wavenumber(h, p):
         return h * HALF + p + 2 * ii
 
-    def table(ref, h, p):
-        start = (2 * h + p) * GPAD
-        return ref[start : start + GPAD, :]
+    def table(p):
+        return trig_t[p * 4 * GPAD : (p + 1) * 4 * GPAD, :]
 
     finish("wave", wave, waves, coef, fx, s1, r1)
-    even = jnp.zeros((2 * rows, kpad), F32)
-    odd = jnp.zeros((2 * rows, kpad), F32)
+    terms = [[[], []], [[], []]]
     for h in range(2):
         here = [fx[w, h * 2 * rows : (h + 1) * 2 * rows, :] for w in range(waves)]
         both = dot_nt(jnp.concatenate(here, axis=1), hot[h])
@@ -148,14 +156,11 @@
             factor = jnp.where(2 * m < n_row, jnp.where(m == 0, 1.0, 2.0), 0.0)
             part = both[:, p * GPAD : (p + 1) * GPAD]
             re, im = part[:rows] * factor, part[rows:] * factor
-            if p == 0:
-                first = jnp.concatenate([re, re * sign]).astype(BF16)
-                other = jnp.concatenate([-im, -im * sign]).astype(BF16)
-                even = even + dot(first, table(cos_t, h, p)) + dot(other, table(sin_t, h, p))
-            else:
-                first = jnp.concatenate([re, im * sign]).astype(BF16)
-                other = jnp.concatenate([-im, re * sign]).astype(BF16)
-                odd = odd + dot(first, table(cos_t, h, p)) + dot(other, table(sin_t, h, p))
+            cos_side, sin_side = ((re, re), (-im, -im)) if p == 0 else ((re, im), (-im, re))
+            for x, (a, b) in enumerate((cos_side, sin_side)):
+                terms[p][x].append(jnp.concatenate([a, b * sign]).astype(BF16))
+    even = dot(jnp.concatenate(terms[0][0] + terms[0][1], axis=1), table(0))
+    odd = dot(jnp.concatenate(terms[1][0] + terms[1][1], axis=1), table(1))
 
     def lat_of(x, v):
         return jnp.where(
@@ -201,9 +206,10 @@
 
     even_in = by_lat((x0 + x2) + (x1 + x3), (x0 + x2) - (x1 + x3))
     odd_in = by_lat(x0 - x2, x1 - x3)
+    even_out, odd_out = dot_nt(even_in, table(0)), dot_nt(odd_in, table(1))
     for h in range(2):
-        ec, es = dot_nt(even_in, table(cos_t, h, 0)), dot_nt(even_in, table(sin_t, h, 0))
-        oc, os_ = dot_nt(odd_in, table(cos_t, h, 1)), dot_nt(odd_in, table(sin_t, h, 1))
+        at_c, at_s = slice(h * GPAD, (h + 1) * GPAD), slice((2 + h) * GPAD, (3 + h) * GPAD)
+        ec, es, oc, os_ = even_out[:, at_c], even_out[:, at_s], odd_out[:, at_c], odd_out[:, at_s]
         keep_e = jnp.where(2 * wavenumber(h, 0) < n_row, weight, 0.0)
         keep_o = jnp.where(2 * wavenumber(h, 1) < n_row, weight, 0.0)
         e_re = jnp.where(up, ec[:rows], ec[rows:]) * keep_e
@@ -238,15 +244,15 @@
             pltpu.VMEM(chunk, BF16), pltpu.VMEM(chunk, BF16),
             pltpu.VMEM(chunk, BF16), pltpu.VMEM(chunk, BF16),
             pltpu.VMEM(coef.shape, BF16),
-            pltpu.VMEM((4 * GPAD, kpad), BF16), pltpu.VMEM((4 * GPAD, kpad), BF16),
-            pltpu.VMEM((4 * BLOCKS + RADIX, kpad), F32),
-            pltpu.VMEM((4 * BLOCKS + RADIX, kpad), F32),
+            pltpu.VMEM((8 * GPAD, kpad), BF16),
+            pltpu.VMEM((4 * SPAN + RADIX, kpad), F32),
+            pltpu.VMEM((4 * SPAN + RADIX, kpad), F32),
             pltpu.VMEM((2, 2 * GPAD, waves * slots), BF16),
             dma((waves,)), dma((waves,)), dma((tiles,)), dma((tiles,)),
             dma((tiles,)), dma((tiles,)), dma((waves,)), dma((waves,)),
         ],
         compiler_params=pltpu.CompilerParams(
-            collective_id=0, has_side_effects=True, vmem_limit_bytes=48 * 2**20
+            collective_id=0, has_side_effects=True, vmem_limit_bytes=60 * 2**20
         ),
         name="middle",
     )(coef, ids)
@@ -255,9 +261,10 @@
 def halves_of(ids, legendre, base, lane):
     parts = []
     for b in range(legendre.shape[0]):
-        block = legendre[b]
-        low = jnp.where(lane < MW - ids[base + b], 1.0, 0.0).astype(BF16) * block
-        parts += [low, block - low]
+        block = legendre[b].astype(F32)
+        low = lane < MW - ids[base + b]
+        both = [jnp.where(low, block, 0.0), jnp.where(low, 0.0, block)]
+        parts.append(jnp.concatenate(both).astype(BF16))
     return jnp.concatenate(parts)
 
 
@@ -276,23 +283,24 @@
     take, lats, row_total = legendre.shape
     fields = spectral.shape[1] * spectral.shape[2]
     base = lax.axis_index("wave") * slots + pl.program_id(0) * take
-    lane = lax.broadcasted_iota(jnp.int32, (1, row_total), 1)
+    lane = lax.broadcasted_iota(jnp.int32, (lats, row_total), 1)
     left = halves_of(ids, legendre, base, lane)
-    right = spectral[...].reshape(take * fields, row_total)
+    right = spectral[...].astype(F32).reshape(take * fields, row_total).astype(BF16)
     full = dot_nt(left, right)
     full = jnp.where(same_slot(full.shape, 2 * lats, fields), full, 0.0).astype(BF16)
-    out[0] = dot(full, fold(take * fields, fields)).astype(BF16)
+    out[...] = dot(full, fold(take * fields, fields)).astype(BF16).reshape(out.shape)
 
 
 def inverse_kernel(slots, ids, back, legendre, out):
     take, lats, row_total = legendre.shape
     fields = out.shape[1] * out.shape[2]
     base = lax.axis_index("wave") * slots + pl.program_id(0) * take
-    lane = lax.broadcasted_iota(jnp.int32, (1, row_total), 1)
+    lane = lax.broadcasted_iota(jnp.int32, (lats, row_total), 1)
     right = halves_of(ids, legendre, base, lane)
-    wide = dot_nt(back[0], fold(take * 2 * lats, 2 * lats))
+    narrow = back[...].reshape(take * fields, 2 * lats)
+    wide = dot_nt(narrow, fold(take * 2 * lats, 2 * lats))
     wide = jnp.where(same_slot(wide.shape, fields, 2 * lats), wide, 0.0).astype(BF16)
-    out[...] = dot(wide, right).astype(BF16).reshape(out.shape)
+    out[...] = dot(wide, right).reshape(out.shape).astype(BF16)
 
 
 def local(spectral, legendre, pair_ids):
@@ -304,28 +312,28 @@
     smem = pl.BlockSpec(memory_space=pltpu.SMEM)
     spec_block = pl.BlockSpec((take, 2, cols, row_total), lambda g: (g, 0, 0, 0))
     leg_block = pl.BlockSpec((take, lat_count, row_total), lambda g: (g, 0, 0))
-    params = pltpu.CompilerParams(vmem_limit_bytes=40 * 2**20)
+    params = pltpu.CompilerParams(vmem_limit_bytes=60 * 2**20)
     coef = pl.pallas_call(
         functools.partial(forward_kernel, slots),
         grid=(groups,),
-        out_shape=jax.ShapeDtypeStruct((groups, take * 2 * lat_count, 2 * cols), BF16),
+        out_shape=jax.ShapeDtypeStruct((slots, 2 * lat_count, 2 * cols), BF16),
         in_specs=[smem, spec_block, leg_block],
-        out_specs=pl.BlockSpec((1, take * 2 * lat_count, 2 * cols), lambda g: (g, 0, 0)),
+        out_specs=pl.BlockSpec((take, 2 * lat_count, 2 * cols), lambda g: (g, 0, 0)),
         compiler_params=params,
         name="forward",
     )(pair_ids, spectral, legendre)
     coef = coef.reshape(slots, 2, waves, 2, 2, cols).transpose(2, 1, 4, 3, 5, 0)
     coef = coef.reshape(waves, 8 * cols, slots)
-    back = middle(coef, pair_ids.reshape(1, PAIRS), waves, tiles, cols, lat_count)
+    back = middle(coef, pair_ids, waves, tiles, cols, lat_count)
     back = back.reshape(waves, 2, 2, 2, cols, slots).transpose(5, 2, 4, 1, 0, 3)
-    back = back.reshape(groups, take * 2 * cols, 2 * lat_count)
+    back = back.reshape(slots, 2 * cols, 2 * lat_count)
     return pl.pallas_call(
         functools.partial(inverse_kernel, slots),
         grid=(groups,),
         out_shape=jax.ShapeDtypeStruct(spectral.shape, BF16),
         in_specs=[
             smem,
-            pl.BlockSpec((1, take * 2 * cols, 2 * lat_count), lambda g: (g, 0, 0)),
+            pl.BlockSpec((take, 2 * cols, 2 * lat_count), lambda g: (g, 0, 0)),
             leg_block,
         ],
         out_specs=spec_block,

time: 55.9 us -> 54.9 us (0.982)
  local copies, waits for them, and re-layouts: 13.7 us -> 4.53 us
  Pallas kernels: 41.9 us -> 49.8 us
    unnamed x10 -> x0, local copies, waits for them, and re-layouts: 7.77 us -> none
    pallas_call x1, Pallas kernels: 6.47 us -> 10.6 us  [local(): pl.pallas_call(functools.partial(forward_kernel, slots), grid=(groups,),...]
    reshape x4 -> x1, local copies, waits for them, and re-layouts: 3.69 us -> 1.37 us  [local(): back = back.reshape(slots, 2 * cols, 2 * lat_count)]
    pallas_call x1, Pallas kernels: 8.11 us -> 10.4 us  [local(): pl.pallas_call(functools.partial(inverse_kernel, slots), grid=(groups,),...]
    pallas_call x0 -> x1, local copies, waits for them, and re-layouts: none -> 1.58 us  [local(): pl.pallas_call(functools.partial(forward_kernel, slots), grid=(groups,),...]
    pallas_call x1, Pallas kernels: 27.3 us -> 28.8 us  [middle(): pl.pallas_call(functools.partial(middle_kernel, waves, tiles, cols, lat_c...]
    transpose x1, local copies, waits for them, and re-layouts: 1.28 us -> 0.67 us  [local(): coef = coef.reshape(slots, 2, waves, 2, 2, cols).transpose(2, 1, 4, 3, 5, 0)]
where the time goes in v4:
time: 54.9 us; the launch traced here: 54.3 us
  Pallas kernels  49.8 us (91%)
  local copies, waits for them, and re-layouts  4.53 us (8%)
    pallas_call x1, Pallas kernels, middle(): pl.pallas_call(functools.partial(middle_kernel, waves, tiles, cols, lat_c...  28.8 us
    pallas_call x1, Pallas kernels, local(): pl.pallas_call(functools.partial(forward_kernel, slots), grid=(groups,),...  10.6 us
    pallas_call x1, Pallas kernels, local(): pl.pallas_call(functools.partial(inverse_kernel, slots), grid=(groups,),...  10.4 us
    pallas_call x1, local copies, waits for them, and re-layouts, local(): pl.pallas_call(functools.partial(forward_kernel, slots), grid=(groups,),...  1.58 us
    reshape x1, local copies, waits for them, and re-layouts, local(): back = back.reshape(slots, 2 * cols, 2 * lat_count)  1.37 us

profile of v4, /device:TPU:0, one launch (start us, length us, event | category | flops | bytes accessed | tf_op | source)
XLA Modules:
  0.0 54.3 jit_solution(8936015851246443826)
XLA Ops:
  0.0 10.6 %forward.1 = bf16[160,16,16]{2,1,0:T(8,128)(2,1)} custom-call(s32[640]{0:T(1024)} %ids.3, bf16[160,2,8,1281]{3,2,1,0:T(8,128)(2,1)} %spectral.1, bf16[160,8,1281]{2,1,0:T(8,128)(2,1)} %legendre.3), custom_call_target="tpu_custom_call" | custom-call | tf_op jit(solution)/shard_map/forward/pallas_call | solution.py:316
  10.6 1.6 %copy.6 = bf16[160,16,16]{0,2,1:T(8,128)(2,1)S(1)} copy(bf16[160,16,16]{2,1,0:T(8,128)(2,1)} %forward.1) | data formatting | bytes 163840 | tf_op jit(solution)/shard_map/forward/pallas_call | solution.py:316
  12.2 0.7 %copy.7 = bf16[4,2,2,2,8,160]{5,4,3,2,1,0:T(8,128)(2,1)} copy(bf16[4,2,2,2,8,160]{5,4,2,3,0,1:T(8,128)(2,1)S(1)} %bitcast.10) | data formatting | bytes 163840 | tf_op jit(solution)/shard_map/transpose | solution.py:325
  12.9 28.8 %middle.1 = bf16[4,64,160]{2,1,0:T(8,128)(2,1)} custom-call(bf16[4,64,160]{2,1,0:T(8,128)(2,1)} %bitcast.8, s32[640]{0:T(1024)} %ids.3), custom_call_target="tpu_custom_call" | custom-call | tf_op jit(solution)/shard_map/middle/pallas_call | solution.py:237
  41.6 0.9 %copy.8 = bf16[4,2,2,2,8,160]{5,4,2,3,0,1:T(8,128)(2,1)S(1)} copy(bf16[4,2,2,2,8,160]{5,4,3,2,1,0:T(8,128)(2,1)} %bitcast.9) | data formatting | bytes 163840 | tf_op jit(solution)/shard_map/reshape | solution.py:328
  42.6 1.4 %copy.9.back = bf16[160,16,16]{2,1,0:T(8,128)(2,1)} copy(bf16[160,16,16]{0,1,2:T(8,128)(2,1)S(1)} %bitcast.11) | data formatting | bytes 163840 | tf_op jit(solution)/shard_map/reshape | solution.py:329
  43.9 10.4 %inverse.1 = bf16[160,2,8,1281]{3,2,1,0:T(8,128)(2,1)} custom-call(s32[640]{0:T(1024)} %ids.3, bf16[160,16,16]{2,1,0:T(8,128)(2,1)} %copy.9.back, bf16[160,8,1281]{2,1,0:T(8,128)(2,1)} %legendre.3), custom_call_target="tpu_custom_call" | custom-call | tf_op jit(solution)/shard_map/inverse/pallas_call | solution.py:330

commit v5 on v4

--- a/solution.py
+++ b/solution.py
@@ -252,18 +252,19 @@
             dma((tiles,)), dma((tiles,)), dma((waves,)), dma((waves,)),
         ],
         compiler_params=pltpu.CompilerParams(
-            collective_id=0, has_side_effects=True, vmem_limit_bytes=60 * 2**20
+            collective_id=0, has_side_effects=True, vmem_limit_bytes=40 * 2**20
         ),
         name="middle",
     )(coef, ids)
 
 
-def halves_of(ids, legendre, base, lane):
+def halves_of(ids, block, base):
+    lane = lax.broadcasted_iota(jnp.int32, block.shape[1:], 1)
     parts = []
-    for b in range(legendre.shape[0]):
-        block = legendre[b].astype(F32)
+    for b in range(block.shape[0]):
+        rows = block[b].astype(F32)
         low = lane < MW - ids[base + b]
-        both = [jnp.where(low, block, 0.0), jnp.where(low, 0.0, block)]
+        both = [jnp.where(low, rows, 0.0), jnp.where(low, 0.0, rows)]
         parts.append(jnp.concatenate(both).astype(BF16))
     return jnp.concatenate(parts)
 
@@ -279,28 +280,59 @@
     return jnp.where(same, 1.0, 0.0).astype(BF16)
 
 
-def forward_kernel(slots, ids, spectral, legendre, out):
-    take, lats, row_total = legendre.shape
+def forward_kernel(take, ids, spectral, legendre, out, spec_v, leg_v, spec_sem, leg_sem):
+    slots, lats, row_total = legendre.shape
     fields = spectral.shape[1] * spectral.shape[2]
-    base = lax.axis_index("wave") * slots + pl.program_id(0) * take
-    lane = lax.broadcasted_iota(jnp.int32, (lats, row_total), 1)
-    left = halves_of(ids, legendre, base, lane)
-    right = spectral[...].astype(F32).reshape(take * fields, row_total).astype(BF16)
-    full = dot_nt(left, right)
-    full = jnp.where(same_slot(full.shape, 2 * lats, fields), full, 0.0).astype(BF16)
-    out[...] = dot(full, fold(take * fields, fields)).astype(BF16).reshape(out.shape)
-
-
-def inverse_kernel(slots, ids, back, legendre, out):
-    take, lats, row_total = legendre.shape
+    base = lax.axis_index("wave") * slots
+    copies = []
+    for g in range(slots // take):
+        at = pl.ds(g * take, take)
+        pair = [
+            pltpu.make_async_copy(legendre.at[at], leg_v.at[at], leg_sem.at[g]),
+            pltpu.make_async_copy(spectral.at[at], spec_v.at[at], spec_sem.at[g]),
+        ]
+        for copy in pair:
+            copy.start()
+        copies.append(pair)
+    shape = (take * 2 * lats, take * fields)
+    same = same_slot(shape, 2 * lats, fields)
+    folded = fold(take * fields, fields)
+    for g, pair in enumerate(copies):
+        for copy in pair:
+            copy.wait()
+        here = slice(g * take, (g + 1) * take)
+        left = halves_of(ids, leg_v[here], base + g * take)
+        right = spec_v[here].astype(F32).reshape(take * fields, row_total).astype(BF16)
+        full = jnp.where(same, dot_nt(left, right), 0.0).astype(BF16)
+        full = dot(full, folded).astype(BF16)
+        out[here] = full.reshape((take,) + out.shape[1:])
+
+
+def inverse_kernel(take, ids, back, legendre, out, leg_v, out_v, leg_sem, out_sem):
+    slots, lats, row_total = legendre.shape
     fields = out.shape[1] * out.shape[2]
-    base = lax.axis_index("wave") * slots + pl.program_id(0) * take
-    lane = lax.broadcasted_iota(jnp.int32, (lats, row_total), 1)
-    right = halves_of(ids, legendre, base, lane)
-    narrow = back[...].reshape(take * fields, 2 * lats)
-    wide = dot_nt(narrow, fold(take * 2 * lats, 2 * lats))
-    wide = jnp.where(same_slot(wide.shape, fields, 2 * lats), wide, 0.0).astype(BF16)
-    out[...] = dot(wide, right).reshape(out.shape).astype(BF16)
+    base = lax.axis_index("wave") * slots
+    copies = []
+    for g in range(slots // take):
+        at = pl.ds(g * take, take)
+        copies.append(pltpu.make_async_copy(legendre.at[at], leg_v.at[at], leg_sem.at[g]))
+        copies[-1].start()
+    shape = (take * fields, take * 2 * lats)
+    same = same_slot(shape, fields, 2 * lats)
+    folded = fold(take * 2 * lats, 2 * lats)
+    results = []
+    for g, copy in enumerate(copies):
+        at = pl.ds(g * take, take)
+        here = slice(g * take, (g + 1) * take)
+        narrow = back[here].reshape(take * fields, 2 * lats)
+        wide = jnp.where(same, dot_nt(narrow, folded), 0.0).astype(BF16)
+        copy.wait()
+        right = halves_of(ids, leg_v[here], base + g * take)
+        out_v[here] = dot(wide, right).reshape((take,) + out.shape[1:]).astype(BF16)
+        results.append(pltpu.make_async_copy(out_v.at[at], out.at[at], out_sem.at[g]))
+        results[-1].start()
+    for copy in results:
+        copy.wait()
 
 
 def local(spectral, legendre, pair_ids):
@@ -310,15 +342,18 @@
     take = max(b for b in range(1, 17) if slots % b == 0)
     groups = slots // take
     smem = pl.BlockSpec(memory_space=pltpu.SMEM)
-    spec_block = pl.BlockSpec((take, 2, cols, row_total), lambda g: (g, 0, 0, 0))
-    leg_block = pl.BlockSpec((take, lat_count, row_total), lambda g: (g, 0, 0))
+    vmem = pl.BlockSpec(memory_space=pltpu.VMEM)
+    hbm = pl.BlockSpec(memory_space=pl.ANY)
+    dma = pltpu.SemaphoreType.DMA((groups,))
     params = pltpu.CompilerParams(vmem_limit_bytes=60 * 2**20)
     coef = pl.pallas_call(
-        functools.partial(forward_kernel, slots),
-        grid=(groups,),
+        functools.partial(forward_kernel, take),
         out_shape=jax.ShapeDtypeStruct((slots, 2 * lat_count, 2 * cols), BF16),
-        in_specs=[smem, spec_block, leg_block],
-        out_specs=pl.BlockSpec((take, 2 * lat_count, 2 * cols), lambda g: (g, 0, 0)),
+        in_specs=[smem, hbm, hbm],
+        out_specs=vmem,
+        scratch_shapes=[
+            pltpu.VMEM(spectral.shape, BF16), pltpu.VMEM(legendre.shape, BF16), dma, dma,
+        ],
         compiler_params=params,
         name="forward",
     )(pair_ids, spectral, legendre)
@@ -328,15 +363,13 @@
     back = back.reshape(waves, 2, 2, 2, cols, slots).transpose(5, 2, 4, 1, 0, 3)
     back = back.reshape(slots, 2 * cols, 2 * lat_count)
     return pl.pallas_call(
-        functools.partial(inverse_kernel, slots),
-        grid=(groups,),
+        functools.partial(inverse_kernel, take),
         out_shape=jax.ShapeDtypeStruct(spectral.shape, BF16),
-        in_specs=[
-            smem,
-            pl.BlockSpec((take, 2 * cols, 2 * lat_count), lambda g: (g, 0, 0)),
-            leg_block,
+        in_specs=[smem, vmem, hbm],
+        out_specs=hbm,
+        scratch_shapes=[
+            pltpu.VMEM(legendre.shape, BF16), pltpu.VMEM(spectral.shape, BF16), dma, dma,
         ],
-        out_specs=spec_block,
         compiler_params=params,
         name="inverse",
     )(pair_ids, back, legendre)

time: 54.9 us -> 48.4 us (0.88)
  Pallas kernels: 49.8 us -> 45 us
  local copies, waits for them, and re-layouts: 4.53 us -> 2.99 us
    pallas_call x2, Pallas kernels: 21 us -> 17.6 us  [the longest x1 10.1 us: local(): pl.pallas_call(functools.partial(forward_kernel, take), out_shape=jax.Sha...]
    pallas_call x1, Pallas kernels: 28.8 us -> 27.5 us  [middle(): pl.pallas_call(functools.partial(middle_kernel, waves, tiles, cols, lat_c...]
    reshape x1, local copies, waits for them, and re-layouts: 0.91 us -> 0.01 us  [local(): back = back.reshape(waves, 2, 2, 2, cols, slots).transpose(5, 2, 4, 1, 0, 3)]
    transpose x1, local copies, waits for them, and re-layouts: 0.67 us -> 0.01 us  [local(): coef = coef.reshape(slots, 2, waves, 2, 2, cols).transpose(2, 1, 4, 3, 5, 0)]
where the time goes in v5:
time: 48.4 us; the launch traced here: 48.2 us
  Pallas kernels  45 us (93%)
  local copies, waits for them, and re-layouts  2.99 us (6%)
    pallas_call x1, Pallas kernels, middle(): pl.pallas_call(functools.partial(middle_kernel, waves, tiles, cols, lat_c...  27.5 us
    pallas_call x1, Pallas kernels, local(): pl.pallas_call(functools.partial(forward_kernel, take), out_shape=jax.Sha...  10.1 us
    pallas_call x1, Pallas kernels, local(): pl.pallas_call(functools.partial(inverse_kernel, take), out_shape=jax.Sha...  7.45 us
    pallas_call x1, local copies, waits for them, and re-layouts, local(): pl.pallas_call(functools.partial(forward_kernel, take), out_shape=jax.Sha...  1.58 us
    reshape x1, local copies, waits for them, and re-layouts, local(): back = back.reshape(slots, 2 * cols, 2 * lat_count)  1.39 us

profile of v5, /device:TPU:0, one launch (start us, length us, event | category | flops | bytes accessed | tf_op | source)
XLA Modules:
  0.0 48.2 jit_solution(13598277528438429335)
XLA Ops:
  0.0 0.0 copy-start
  0.0 10.1 %forward.1 = bf16[160,16,16]{2,1,0:T(8,128)(2,1)} custom-call(s32[640]{0:T(1024)} %ids.3, bf16[160,2,8,1281]{3,2,1,0:T(8,128)(2,1)} %spectral.1, bf16[160,8,1281]{2,1,0:T(8,128)(2,1)} %legendre.3), custom_call_target="tpu_custom_call" | custom-call | tf_op jit(solution)/shard_map/forward/pallas_call | solution.py:349
  10.1 1.6 %copy.6 = bf16[160,16,16]{0,2,1:T(8,128)(2,1)S(1)} copy(bf16[160,16,16]{2,1,0:T(8,128)(2,1)} %forward.1) | data formatting | bytes 163840 | tf_op jit(solution)/shard_map/forward/pallas_call | solution.py:349
  11.7 0.0 copy-done
  11.8 27.5 %middle.1 = bf16[4,64,160]{2,1,0:T(8,128)(2,1)S(1)} custom-call(bf16[4,64,160]{2,1,0:T(8,128)(2,1)S(1)} %bitcast.8, s32[640]{0:T(1024)S(1)} %copy-done), custom_call_target="tpu_custom_call" | custom-call | tf_op jit(solution)/shard_map/middle/pallas_call | solution.py:237
  39.2 1.4 %copy.9.back = bf16[160,16,16]{2,1,0:T(8,128)(2,1)} copy(bf16[160,16,16]{0,1,2:T(8,128)(2,1)S(1)} %bitcast.11) | data formatting | bytes 163840 | tf_op jit(solution)/shard_map/reshape | solution.py:364
  40.6 7.4 %inverse.1 = bf16[160,2,8,1281]{3,2,1,0:T(8,128)(2,1)} custom-call(s32[640]{0:T(1024)} %ids.3, bf16[160,16,16]{2,1,0:T(8,128)(2,1)} %copy.9.back, bf16[160,8,1281]{2,1,0:T(8,128)(2,1)} %legendre.3), custom_call_target="tpu_custom_call" | custom-call | tf_op jit(solution)/shard_map/inverse/pallas_call | solution.py:365
  (2 shorter events, 0.0 us)
Async XLA Ops:
  0.0 11.7 %copy-start = (s32[640]{0:T(1024)S(1)}, s32[640]{0:T(1024)}, u32[]{:S(2)}) copy-start(s32[640]{0:T(1024)} %ids.3) | copy-start | bytes 7684

commit v6 on v5

--- a/solution.py
+++ b/solution.py
@@ -23,6 +23,7 @@
 GPAD = -(-GROUP // LANES) * LANES
 BLOCKS = GPAD // RADIX
 SPAN = 16
+AHEAD = 3
 MESH = pl.DeviceIdType.MESH
 NT = (((1,), (1,)), ((), ()))
 
@@ -72,8 +73,6 @@
             pl.semaphore_signal(
                 barrier, inc=1, device_id={axis: lax.rem(here + off, count)}, device_id_type=MESH
             )
-    pl.semaphore_wait(barrier, waves + tiles - 2)
-    sends = exchange("wave", wave, waves, coef, fx, s1, r1)
 
     polar = wave * HALF // (lat_count // 2)
     q0 = 5 + polar
@@ -107,6 +106,9 @@
         ca, sa, cb, sb = c[:8], s[:8], c[8 + g : 9 + g], s[8 + g : 9 + g]
         small_c[outer + 8 * g : outer + 8 * g + 8] = ca * cb - sa * sb
         small_s[outer + 8 * g : outer + 8 * g + 8] = sa * cb + ca * sb
+
+    pl.semaphore_wait(barrier, waves + tiles - 2)
+    sends = exchange("wave", wave, waves, coef, fx, s1, r1)
 
     def block(idx, carry):
         g, a = idx // BLOCKS, idx % BLOCKS
@@ -291,15 +293,18 @@
             pltpu.make_async_copy(legendre.at[at], leg_v.at[at], leg_sem.at[g]),
             pltpu.make_async_copy(spectral.at[at], spec_v.at[at], spec_sem.at[g]),
         ]
+        copies.append(pair)
+    for pair in copies[:AHEAD]:
         for copy in pair:
             copy.start()
-        copies.append(pair)
     shape = (take * 2 * lats, take * fields)
     same = same_slot(shape, 2 * lats, fields)
     folded = fold(take * fields, fields)
     for g, pair in enumerate(copies):
         for copy in pair:
             copy.wait()
+        for copy in copies[g + AHEAD] if g + AHEAD < len(copies) else ():
+            copy.start()
         here = slice(g * take, (g + 1) * take)
         left = halves_of(ids, leg_v[here], base + g * take)
         right = spec_v[here].astype(F32).reshape(take * fields, row_total).astype(BF16)

time: 48.4 us -> 48.1 us (level)
  no operation moved by 1% of the time
where the time goes in v6:
time: 48.1 us; the launch traced here: 47.9 us
  Pallas kernels  44.7 us (93%)
  local copies, waits for them, and re-layouts  2.99 us (6%)
    pallas_call x1, Pallas kernels, middle(): pl.pallas_call(functools.partial(middle_kernel, waves, tiles, cols, lat_c...  27.1 us
    pallas_call x1, Pallas kernels, local(): pl.pallas_call(functools.partial(forward_kernel, take), out_shape=jax.Sha...  10.1 us
    pallas_call x1, Pallas kernels, local(): pl.pallas_call(functools.partial(inverse_kernel, take), out_shape=jax.Sha...  7.44 us
    pallas_call x1, local copies, waits for them, and re-layouts, local(): pl.pallas_call(functools.partial(forward_kernel, take), out_shape=jax.Sha...  1.58 us
    reshape x1, local copies, waits for them, and re-layouts, local(): back = back.reshape(slots, 2 * cols, 2 * lat_count)  1.39 us

profile of v6, /device:TPU:0, one launch (start us, length us, event | category | flops | bytes accessed | tf_op | source)
XLA Modules:
  0.0 47.9 jit_solution(8788842695093645115)
XLA Ops:
  0.0 0.0 copy-start
  0.0 10.1 %forward.1 = bf16[160,16,16]{2,1,0:T(8,128)(2,1)} custom-call(s32[640]{0:T(1024)} %ids.3, bf16[160,2,8,1281]{3,2,1,0:T(8,128)(2,1)} %spectral.1, bf16[160,8,1281]{2,1,0:T(8,128)(2,1)} %legendre.3), custom_call_target="tpu_custom_call" | custom-call | tf_op jit(solution)/shard_map/forward/pallas_call | solution.py:354
  10.2 1.6 %copy.6 = bf16[160,16,16]{0,2,1:T(8,128)(2,1)S(1)} copy(bf16[160,16,16]{2,1,0:T(8,128)(2,1)} %forward.1) | data formatting | bytes 163840 | tf_op jit(solution)/shard_map/forward/pallas_call | solution.py:354
  11.8 0.0 copy-done
  11.8 27.1 %middle.1 = bf16[4,64,160]{2,1,0:T(8,128)(2,1)S(1)} custom-call(bf16[4,64,160]{2,1,0:T(8,128)(2,1)S(1)} %bitcast.8, s32[640]{0:T(1024)S(1)} %copy-done), custom_call_target="tpu_custom_call" | custom-call | tf_op jit(solution)/shard_map/middle/pallas_call | solution.py:239
  38.9 1.4 %copy.9.back = bf16[160,16,16]{2,1,0:T(8,128)(2,1)} copy(bf16[160,16,16]{0,1,2:T(8,128)(2,1)S(1)} %bitcast.11) | data formatting | bytes 163840 | tf_op jit(solution)/shard_map/reshape | solution.py:369
  40.3 7.4 %inverse.1 = bf16[160,2,8,1281]{3,2,1,0:T(8,128)(2,1)} custom-call(s32[640]{0:T(1024)} %ids.3, bf16[160,16,16]{2,1,0:T(8,128)(2,1)} %copy.9.back, bf16[160,8,1281]{2,1,0:T(8,128)(2,1)} %legendre.3), custom_call_target="tpu_custom_call" | custom-call | tf_op jit(solution)/shard_map/inverse/pallas_call | solution.py:370
  (2 shorter events, 0.0 us)
Async XLA Ops:
  0.0 11.8 %copy-start = (s32[640]{0:T(1024)S(1)}, s32[640]{0:T(1024)}, u32[]{:S(2)}) copy-start(s32[640]{0:T(1024)} %ids.3) | copy-start | bytes 7684
